TPU v7x, 1024 devices: a whole 4x8x16 slice. The times are simulated.
1024 devices in a mesh: dp: 16 (over z), fsdp: 4 (over x), expert: 16 (over y, core).
Axes of the slice: x: 4, y: 8, z: 16, core: 2. Of those that a mesh axis runs over, the one named last changes fastest.
Arguments:
- tokens: bfloat16 [32768, 4096], P(('dp', 'expert'), 'fsdp'), may hold values from -24 to 24
- cotangent: bfloat16 [32768, 4096], P(('dp', 'expert'), 'fsdp'), may hold values from -6 to 6
- routes: int32 [32768, 8], P(('dp', 'expert')), may hold values from 0 to 127, as said below
- route_gates: float32 [32768, 8], P(('dp', 'expert')), may hold values from 0.05 to 0.6
- gate_weight: bfloat16 [16, 4096, 768], P('expert', None, 'fsdp'), may hold values from -0.09375 to 0.09375
- up_weight: bfloat16 [16, 4096, 768], P('expert', None, 'fsdp'), may hold values from -0.09375 to 0.09375
- down_weight: bfloat16 [16, 768, 4096], P('expert', 'fsdp'), may hold values from -0.21875 to 0.21875
Outputs:
- token_grads: bfloat16 [32768, 4096], P(('dp', 'expert'), 'fsdp')
- gate_grads: bfloat16 [16, 4096, 768], P('expert', 'dp', 'fsdp')
- up_grads: bfloat16 [16, 4096, 768], P('expert', 'dp', 'fsdp')
- down_grads: bfloat16 [16, 768, 4096], P('expert', 'fsdp', 'dp')
Inputs may be any that keep to these rules, and one draw needn't show every extreme that they name: `routes`: each token names 8 different ids, exactly one in each run of 16 ids (0 to 15, 16 to 31, and so on). In each aligned block of 128 tokens (one index of dp and expert together) no id below 16 is named by more than 10 tokens, and in every draw one id below 16 is named by exactly 10 tokens of every block.
All inputs are finite; a program needn't handle non-finite values.
Results may differ from a plain program's by a relative error of at most 0.017.
Values may be sent and summed in bfloat16 or wider, within the bound.
No kernel may reach another device: no remote copies, remote signals or barrier semaphores. Data moves between devices by JAX's collectives and lax.ppermute only.
A program may use at most 32 MiB of HBM per device.

v0:
```python
import jax
import jax.numpy as jnp
from jax import lax
from jax.sharding import PartitionSpec as P

CAP = 10


def local(tokens, cotangent, routes, route_gates, gate_weight, up_weight, down_weight):
    owners = lax.axis_size("expert")
    quarter = tokens.shape[1]
    in_window = routes < owners
    target = jnp.where(
        jnp.any(in_window, axis=1), jnp.sum(jnp.where(in_window, routes, 0), axis=1), owners
    )
    route_gate = jnp.sum(jnp.where(in_window, route_gates, jnp.float32(0.0)), axis=1)
    scaled = (route_gate[:, None] * cotangent.astype(jnp.float32)).astype(jnp.bfloat16)
    onehot = (target[:, None] == jnp.arange(owners, dtype=jnp.int32)[None, :]).astype(jnp.int32)
    before = jnp.cumsum(onehot, axis=0) - onehot
    position = target * CAP + jnp.sum(before * onehot, axis=1)
    slot_count = owners * CAP
    selector = (jnp.arange(slot_count, dtype=jnp.int32)[:, None] == position[None, :]).astype(
        jnp.bfloat16
    )
    send_rows = (
        jnp.dot(selector, tokens, preferred_element_type=jnp.float32)
        .astype(jnp.bfloat16)
        .reshape(owners, CAP, quarter)
    )
    send_grads = (
        jnp.dot(selector, scaled, preferred_element_type=jnp.float32)
        .astype(jnp.bfloat16)
        .reshape(owners, CAP, quarter)
    )
    recv_rows, recv_grads = (
        lax.all_to_all(send_rows, "expert", split_axis=0, concat_axis=0, tiled=True),
        lax.all_to_all(send_grads, "expert", split_axis=0, concat_axis=0, tiled=True),
    )
    flat_rows = recv_rows.reshape(slot_count, quarter)
    flat_grads = recv_grads.reshape(slot_count, quarter)
    full_rows, full_grads = (
        lax.all_gather(flat_rows, "fsdp", axis=1, tiled=True),
        lax.all_gather(flat_grads, "fsdp", axis=1, tiled=True),
    )
    gate_mat = gate_weight[0]
    up_mat = up_weight[0]
    down_mat = down_weight[0]
    across = (((1,), (1,)), ((), ()))
    gate_pre = jnp.dot(full_rows, gate_mat, preferred_element_type=jnp.float32)
    up_pre = jnp.dot(full_rows, up_mat, preferred_element_type=jnp.float32)
    sigmoid_gate = jax.nn.sigmoid(gate_pre)
    activated = gate_pre * sigmoid_gate
    hidden = (activated * up_pre).astype(jnp.bfloat16)
    hidden_grad = lax.dot_general(full_grads, down_mat, across, preferred_element_type=jnp.float32)
    gate_grad = (
        hidden_grad * up_pre * sigmoid_gate * (1.0 + gate_pre * (1.0 - sigmoid_gate))
    ).astype(jnp.bfloat16)
    up_grad = (hidden_grad * activated).astype(jnp.bfloat16)
    partial_value = lax.dot_general(gate_grad, gate_mat, across, preferred_element_type=jnp.float32)
    partial_value = partial_value + lax.dot_general(
        up_grad, up_mat, across, preferred_element_type=jnp.float32
    )
    route_rows = lax.psum_scatter(
        partial_value.astype(jnp.bfloat16), "fsdp", scatter_dimension=1, tiled=True
    )
    returned = lax.all_to_all(
        route_rows.reshape(owners, CAP, quarter), "expert", split_axis=0, concat_axis=0, tiled=True
    )
    token_grads = lax.dot_general(
        selector,
        returned.reshape(slot_count, quarter),
        (((0,), (0,)), ((), ())),
        preferred_element_type=jnp.float32,
    ).astype(jnp.bfloat16)
    contract = (((0,), (0,)), ((), ()))
    term_gate = lax.dot_general(full_rows, gate_grad, contract, preferred_element_type=jnp.float32)
    term_up = lax.dot_general(full_rows, up_grad, contract, preferred_element_type=jnp.float32)
    term_down = lax.dot_general(full_grads, hidden, contract, preferred_element_type=jnp.float32)
    sum_gate, sum_up, sum_down = (
        lax.psum_scatter(
            term_gate.astype(jnp.bfloat16), "dp", scatter_dimension=0, tiled=True
        ).astype(jnp.float32),
        lax.psum_scatter(
            term_up.astype(jnp.bfloat16), "dp", scatter_dimension=0, tiled=True
        ).astype(jnp.float32),
        lax.psum_scatter(
            term_down.astype(jnp.bfloat16), "dp", scatter_dimension=0, tiled=True
        ).astype(jnp.float32),
    )
    gate_grads = sum_gate.astype(jnp.bfloat16)[None]
    up_grads = sum_up.astype(jnp.bfloat16)[None]
    down_grads = sum_down.astype(jnp.bfloat16).T[None]
    return (token_grads, gate_grads, up_grads, down_grads)


def solution(mesh):
    placed = (
        P(("dp", "expert"), "fsdp"),
        P(("dp", "expert"), "fsdp"),
        P(("dp", "expert"), None),
        P(("dp", "expert"), None),
        P("expert", None, "fsdp"),
        P("expert", None, "fsdp"),
        P("expert", "fsdp", None),
    )
    return jax.shard_map(
        local,
        mesh=mesh,
        in_specs=placed,
        out_specs=(
            P(("dp", "expert"), "fsdp"),
            P("expert", "dp", "fsdp"),
            P("expert", "dp", "fsdp"),
            P("expert", "fsdp", "dp"),
        ),
        check_vma=False,
    )
```

profile of v0, /device:TPU:4, one launch (start us, length us, event | category | flops | bytes accessed | tf_op | source)
XLA Modules:
  0.0 398.1 jit_solution(4536490516954807905)
XLA Ops:
  7.2 0.8 select_reduce_fusion.2
  8.0 0.7 fusion.18
  9.2 1.2 convolution_convert_fusion.3
  10.6 22.9 %all_to_all.15 = bf16[16,10,1024]{2,1,0:T(8,128)(2,1)S(1)} all-to-all(bf16[16,10,1024]{2,1,0:T(8,128)(2,1)S(1)} %reshape.43), channel_id=1, replica_groups=mesh['dp'=16,'fsdp'=4,'expert'=16] {'expert'}, dimensions={0} | all-to-all | bytes 655360 | tf_op jit(solution)/shard_map/all_to_all | solution.py:36
  33.5 0.9 reshape.44
  34.9 20.0 %all_to_all.16 = bf16[16,10,1024]{2,1,0:T(8,128)(2,1)S(1)} all-to-all(bf16[16,10,1024]{2,1,0:T(8,128)(2,1)S(1)} %reshape.41), channel_id=1, replica_groups=mesh['dp'=16,'fsdp'=4,'expert'=16] {'expert'}, dimensions={0} | all-to-all | bytes 655360 | tf_op jit(solution)/shard_map/all_to_all | solution.py:37
  54.9 0.8 reshape.42
  55.8 18.2 %all-gather.5.cloned.1.call-done = bf16[160,4096]{1,0:T(8,128)(2,1)} async-done(((bf16[160,1024]{1,0:T(8,128)(2,1)}), bf16[160,4096]{1,0:T(8,128)(2,1)}) %all-gather.5.cloned.1.call-update) | async-done | bytes 1310736 | tf_op jit(solution)/shard_map/all_gather | solution.py:42
  74.1 2.1 fusion.3
  76.1 2.0 fusion.6
  78.2 34.9 %all-gather.3.cloned.1.call-done = bf16[160,4096]{1,0:T(8,128)(2,1)} async-done(((bf16[160,1024]{1,0:T(8,128)(2,1)}), bf16[160,4096]{1,0:T(8,128)(2,1)}) %all-gather.3.cloned.1.call-update) | async-done | bytes 1310736 | tf_op jit(solution)/shard_map/all_gather | solution.py:43
  113.0 2.5 multiply_convert_fusion.3
  116.0 0.9 copy-done.2
  116.9 1.6 fusion
  118.6 3.1 convolution_convert_fusion
  121.8 1.8 convolution_convert_fusion.1
  123.6 1.8 convolution_convert_fusion.2
  125.4 28.7 %reduce-scatter.5.cloned.1.call-done = bf16[160,1024]{1,0:T(8,128)(2,1)} async-done(((bf16[160,4096]{1,0:T(8,128)(2,1)}), bf16[160,1024]{1,0:T(8,128)(2,1)}) %reduce-scatter.5.cloned.1.call-update) | async-done | bytes 327696 | tf_op jit(solution)/shard_map/reduce_scatter | solution.py:63
  154.1 1.1 reshape.45
  155.2 22.5 %all_to_all.17 = bf16[16,10,1024]{2,1,0:T(8,128)(2,1)S(1)} all-to-all(bf16[16,10,1024]{2,1,0:T(8,128)(2,1)S(1)} %reshape.45), channel_id=1, replica_groups=mesh['dp'=16,'fsdp'=4,'expert'=16] {'expert'}, dimensions={0} | all-to-all | bytes 655360 | tf_op jit(solution)/shard_map/all_to_all | solution.py:66
  177.8 1.0 convolution_convert_fusion.5
  178.8 57.3 %reduce-scatter.11.cloned.1.call-done = bf16[256,192]{0,1:T(8,128)(2,1)} async-done(((bf16[4096,192]{0,1:T(8,128)(2,1)}), bf16[256,192]{0,1:T(8,128)(2,1)}) %reduce-scatter.11.cloned.1.call-update) | async-done | bytes 98320 | tf_op jit(solution)/shard_map/reduce_scatter | solution.py:86
  236.1 77.6 %reduce-scatter.9.cloned.1.call-done = bf16[256,192]{0,1:T(8,128)(2,1)} async-done(((bf16[4096,192]{0,1:T(8,128)(2,1)}), bf16[256,192]{0,1:T(8,128)(2,1)}) %reduce-scatter.9.cloned.1.call-update) | async-done | bytes 98320 | tf_op jit(solution)/shard_map/reduce_scatter | solution.py:83
  313.7 77.5 %reduce-scatter.7.cloned.1.call-done = bf16[256,192]{0,1:T(8,128)(2,1)} async-done(((bf16[4096,192]{0,1:T(8,128)(2,1)}), bf16[256,192]{0,1:T(8,128)(2,1)}) %reduce-scatter.7.cloned.1.call-update) | async-done | bytes 98320 | tf_op jit(solution)/shard_map/reduce_scatter | solution.py:80
  (34 shorter events, 2.0 us)
Async XLA Ops:
  7.2 66.9 %copy-start = (bf16[1,4096,192]{1,2,0:T(8,128)(2,1)S(1)}, bf16[1,4096,192]{1,2,0:T(8,128)(2,1)}, u32[]{:S(2)}) copy-start(bf16[1,4096,192]{1,2,0:T(8,128)(2,1)} %param.11) | copy-start | bytes 4718596
  7.2 66.9 %all-gather.5.cloned.1.call-start = ((), (), s32[]{:S(2)}) async-start(), calls=%async_computation.8 | async-start | bytes 1638400 | tf_op jit(solution)/shard_map/all_gather | solution.py:42
  10.4 24.0 %copy-start.4 = (s32[128,8]{0,1:T(8,128)S(1)}, s32[128,8]{0,1:T(8,128)}, u32[]{:S(2)}) copy-start(s32[128,8]{0,1:T(8,128)} %param.9) | copy-start | bytes 12292
  10.4 24.0 %copy-start.5 = (f32[128,8]{0,1:T(8,128)S(1)}, f32[128,8]{0,1:T(8,128)}, u32[]{:S(2)}) copy-start(f32[128,8]{0,1:T(8,128)} %param.10) | copy-start | bytes 12292
  10.4 24.1 %copy-start.3 = (bf16[128,1024]{1,0:T(8,128)(2,1)S(1)}, bf16[128,1024]{1,0:T(8,128)(2,1)}, u32[]{:S(2)}) copy-start(bf16[128,1024]{1,0:T(8,128)(2,1)} %param.8) | copy-start | bytes 786436
  34.4 78.7 %all-gather.3.cloned.1.call-start = ((), (), s32[]{:S(2)}) async-start(), calls=%async_computation.7 | async-start | bytes 1638400 | tf_op jit(solution)/shard_map/all_gather | solution.py:43
  55.8 98.3 %reduce-scatter.5.cloned.1.call-start = ((), (), s32[]{:S(2)}) async-start(), calls=%async_computation.9 | async-start | bytes 1638400 | tf_op jit(solution)/shard_map/reduce_scatter | solution.py:63
  74.1 2.1 copy-start.1
  115.5 1.4 copy-start.2
  118.6 117.5 %reduce-scatter.11.cloned.1.call-start = ((), (), s32[]{:S(2)}) async-start(), calls=%async_computation.12 | async-start | bytes 1671168 | tf_op jit(solution)/shard_map/reduce_scatter | solution.py:86
  121.8 192.0 %reduce-scatter.9.cloned.1.call-start = ((), (), s32[]{:S(2)}) async-start(), calls=%async_computation.11 | async-start | bytes 1671168 | tf_op jit(solution)/shard_map/reduce_scatter | solution.py:83
  123.6 267.6 %reduce-scatter.7.cloned.1.call-start = ((), (), s32[]{:S(2)}) async-start(), calls=%async_computation.10 | async-start | bytes 1671168 | tf_op jit(solution)/shard_map/reduce_scatter | solution.py:80
Sparse Core Ops, SparseCore 0:
  34.5 39.5 all-gather.4
  76.7 36.2 all-gather.2
  118.7 35.3 reduce-scatter.4
  157.9 78.1 reduce-scatter.10
  239.9 73.7 reduce-scatter.8
  317.6 73.6 reduce-scatter.6
where the time goes:
time: 399 us; the launch traced here: 398 us
  waiting for transfers between devices  294 us (74%)
  blocking collectives  65.5 us (16%)
  matrix products  17.8 us (4%)
  between operations  14.3 us (4%)
  local copies, waits for them, and re-layouts  4.06 us (1%)
    reduce_scatter x1, waiting for transfers between devices, local(): lax.psum_scatter(term_up.astype(jnp.bfloat16), 'dp', scatter_dimension=0,...  77.6 us
    reduce_scatter x1, waiting for transfers between devices, local(): lax.psum_scatter(term_gate.astype(jnp.bfloat16), 'dp', scatter_dimension=...  77.5 us
    reduce_scatter x1, waiting for transfers between devices, local(): lax.psum_scatter(term_down.astype(jnp.bfloat16), 'dp', scatter_dimension=...  57.3 us
    all_gather x1, waiting for transfers between devices, local(): lax.all_gather(flat_grads, 'fsdp', axis=1, tiled=True)  34.9 us
    reduce_scatter x1, waiting for transfers between devices, local(): lax.psum_scatter(partial_value.astype(jnp.bfloat16), 'fsdp', scatter_dime...  28.7 us
    all_to_all x1, blocking collectives, local(): lax.all_to_all(send_rows, 'expert', split_axis=0, concat_axis=0, tiled=True)  22.9 us
    all_to_all x1, blocking collectives, local(): lax.all_to_all(route_rows.reshape(owners, CAP, quarter), 'expert', split_...  22.5 us
    all_to_all x1, blocking collectives, local(): lax.all_to_all(send_grads, 'expert', split_axis=0, concat_axis=0, tiled=T...  20 us
  transfers between devices with their start and end apart: 6, of which 6 were waited for; matrix products, arithmetic and copies ran while one was open for 4% of the time, Pallas kernels for 0%

commit v1 on v0

v1 whole, which is shorter than its diff:
```python
import jax
import jax.numpy as jnp
from jax import lax
from jax.sharding import PartitionSpec as P

CAP = 10
MAIN = 8
TAIL = CAP - MAIN


def packed(values, main_pick, tail_picks):
    pieces = len(tail_picks)
    width = values.shape[1] // pieces
    main = jnp.dot(main_pick, values, preferred_element_type=jnp.float32)
    stacked = jnp.concatenate([values[:, p * width : (p + 1) * width] for p in range(pieces)], 0)
    tail = jnp.dot(
        jnp.concatenate(tail_picks, axis=1), stacked, preferred_element_type=jnp.float32
    )
    return jnp.concatenate([main.astype(jnp.bfloat16), tail.astype(jnp.bfloat16)], axis=1)


def unpacked(received, quarter):
    owners = received.shape[0]
    main = received[:, :, :quarter].reshape(owners * MAIN, quarter)
    tail = received[:, :, quarter:].reshape(owners * TAIL, quarter)
    return jnp.concatenate([main, tail], axis=0)


def local(tokens, cotangent, routes, route_gates, gate_weight, up_weight, down_weight):
    owners = lax.axis_size("expert")
    quarters = lax.axis_size("fsdp")
    quarter = tokens.shape[1]
    pieces = MAIN // TAIL
    in_window = routes < owners
    target = jnp.sum(jnp.where(in_window, routes, 0), axis=1)
    route_gate = jnp.sum(jnp.where(in_window, route_gates, jnp.float32(0.0)), axis=1)
    scaled = (route_gate[:, None] * cotangent.astype(jnp.float32)).astype(jnp.bfloat16)
    onehot = (target[:, None] == jnp.arange(owners, dtype=jnp.int32)[None, :]).astype(jnp.bfloat16)
    count = tokens.shape[0]
    earlier = (
        jnp.arange(count)[:, None] > jnp.arange(count)[None, :]
    ).astype(jnp.bfloat16)
    before = jnp.dot(earlier, onehot, preferred_element_type=jnp.float32)
    rank = jnp.sum(before * onehot.astype(jnp.float32), axis=1).astype(jnp.int32)
    row = jnp.arange(owners * MAIN, dtype=jnp.int32)[:, None]
    owner_row, place = row // MAIN, row % MAIN
    to_owner = owner_row == target[None, :]
    main_pick = (to_owner & (place == rank[None, :])).astype(jnp.bfloat16)
    in_tail = to_owner & (place // pieces + MAIN == rank[None, :])
    tail_picks = [(in_tail & (place % pieces == p)).astype(jnp.bfloat16) for p in range(pieces)]
    shape = (owners, MAIN, quarter + quarter // pieces)
    send_rows = packed(tokens, main_pick, tail_picks).reshape(shape)
    recv_rows = lax.all_to_all(send_rows, "expert", split_axis=0, concat_axis=0, tiled=True)
    send_grads = packed(scaled, main_pick, tail_picks).reshape(shape)
    recv_rows, send_grads = lax.optimization_barrier((recv_rows, send_grads))
    recv_grads = lax.all_to_all(send_grads, "expert", split_axis=0, concat_axis=0, tiled=True)
    full_rows = lax.all_gather(unpacked(recv_rows, quarter), "fsdp", axis=1, tiled=True)
    flat_grads = unpacked(recv_grads, quarter)
    slot_count = flat_grads.shape[0]
    grad_blocks = lax.all_to_all(
        jnp.broadcast_to(flat_grads[None], (quarters, slot_count, quarter)),
        "fsdp",
        split_axis=0,
        concat_axis=0,
        tiled=True,
    )
    full_grads = jnp.concatenate([grad_blocks[k] for k in range(quarters)], axis=1)
    gate_mat = gate_weight[0]
    up_mat = up_weight[0]
    down_mat = down_weight[0]
    across = (((1,), (1,)), ((), ()))
    gate_pre = jnp.dot(full_rows, gate_mat, preferred_element_type=jnp.float32)
    up_pre = jnp.dot(full_rows, up_mat, preferred_element_type=jnp.float32)
    sigmoid_gate = jax.nn.sigmoid(gate_pre)
    activated = gate_pre * sigmoid_gate
    hidden = (activated * up_pre).astype(jnp.bfloat16)
    hidden_grad = lax.dot_general(full_grads, down_mat, across, preferred_element_type=jnp.float32)
    gate_grad = (
        hidden_grad * up_pre * sigmoid_gate * (1.0 + gate_pre * (1.0 - sigmoid_gate))
    ).astype(jnp.bfloat16)
    up_grad = (hidden_grad * activated).astype(jnp.bfloat16)
    contract = (((0,), (0,)), ((), ()))
    gate_up = jnp.concatenate([gate_grad, up_grad], axis=1)
    term_gate_up = lax.dot_general(gate_up, full_rows, contract, preferred_element_type=jnp.float32)
    term_down = lax.dot_general(hidden, full_grads, contract, preferred_element_type=jnp.float32)
    terms = jnp.concatenate(
        [term_gate_up.astype(jnp.bfloat16), term_down.astype(jnp.bfloat16)], axis=0
    )
    sums = lax.psum_scatter(terms, "dp", scatter_dimension=1, tiled=True)
    partial_value = lax.dot_general(gate_grad, gate_mat, across, preferred_element_type=jnp.float32)
    partial_value = partial_value + lax.dot_general(
        up_grad, up_mat, across, preferred_element_type=jnp.float32
    )
    blocks = partial_value.astype(jnp.bfloat16)
    blocks = jnp.stack([blocks[:, k * quarter : (k + 1) * quarter] for k in range(quarters)])
    given = lax.all_to_all(blocks, "fsdp", split_axis=0, concat_axis=0, tiled=True)
    route_rows = (
        given[0].astype(jnp.float32)
        + given[1].astype(jnp.float32)
        + given[2].astype(jnp.float32)
        + given[3].astype(jnp.float32)
    ).astype(jnp.bfloat16)
    mains = owners * MAIN
    returned = lax.all_to_all(
        jnp.concatenate(
            [
                route_rows[:mains].reshape(owners, MAIN, quarter),
                route_rows[mains:].reshape(owners, TAIL, quarter),
            ],
            axis=1,
        ),
        "expert",
        split_axis=0,
        concat_axis=0,
        tiled=True,
    )
    slot = jnp.arange(slot_count, dtype=jnp.int32)[None, :]
    selector = (slot == (target * CAP + rank)[:, None]).astype(jnp.bfloat16)
    token_grads = jnp.dot(
        selector, returned.reshape(slot_count, quarter), preferred_element_type=jnp.float32
    ).astype(jnp.bfloat16)
    width = gate_mat.shape[1]
    return (
        token_grads,
        sums[:width].T[None],
        sums[width : 2 * width].T[None],
        sums[2 * width :][None],
    )


def solution(mesh):
    placed = (
        P(("dp", "expert"), "fsdp"),
        P(("dp", "expert"), "fsdp"),
        P(("dp", "expert"), None),
        P(("dp", "expert"), None),
        P("expert", None, "fsdp"),
        P("expert", None, "fsdp"),
        P("expert", "fsdp", None),
    )
    return jax.shard_map(
        local,
        mesh=mesh,
        in_specs=placed,
        out_specs=(
            P(("dp", "expert"), "fsdp"),
            P("expert", "dp", "fsdp"),
            P("expert", "dp", "fsdp"),
            P("expert", "fsdp", "dp"),
        ),
        check_vma=False,
    )
```

time: 399 us -> 189 us (0.47)
  the two profiles are of different devices: /device:TPU:4 before, /device:TPU:8 now
where the time goes in v1:
time: 189 us; the launch traced here: 188 us
  waiting for transfers between devices  74.7 us (40%)
  blocking collectives  48.2 us (26%)
  starting transfers between devices  27.6 us (15%)
  between operations  14.4 us (8%)
  matrix products  9.14 us (5%)
  other arithmetic  7.4 us (4%)
  local copies, waits for them, and re-layouts  6.46 us (3%)
    reduce_scatter x1, waiting for transfers between devices, local(): sums = lax.psum_scatter(terms, 'dp', scatter_dimension=1, tiled=True)  38.2 us
    all_to_all x1, blocking collectives, local(): lax.all_to_all(jnp.broadcast_to(flat_grads[None], (quarters, slot_count,...  27.5 us
    all_to_all x1, blocking collectives, local(): lax.all_to_all(blocks, 'fsdp', split_axis=0, concat_axis=0, tiled=True)  20.6 us
    all_to_all x1, starting transfers between devices, local(): lax.all_to_all(send_rows, 'expert', split_axis=0, concat_axis=0, tiled=True)  16.4 us
    all_to_all x1, waiting for transfers between devices, local(): lax.all_to_all(jnp.concatenate([route_rows[:mains].reshape(owners, MAIN,...  14.2 us
    all_to_all x1, waiting for transfers between devices, local(): lax.all_to_all(send_grads, 'expert', split_axis=0, concat_axis=0, tiled=T...  9.92 us
    all_to_all x1, waiting for transfers between devices, local(): lax.all_to_all(send_rows, 'expert', split_axis=0, concat_axis=0, tiled=True)  9.3 us
    all_to_all x1, starting transfers between devices, local(): lax.all_to_all(jnp.concatenate([route_rows[:mains].reshape(owners, MAIN,...  5.9 us
  transfers between devices with their start and end apart: 5, of which 5 were waited for; matrix products, arithmetic and copies ran while one was open for 4% of the time, Pallas kernels for 0%

profile of v1, /device:TPU:8, one launch (start us, length us, event | category | flops | bytes accessed | tf_op | source)
XLA Modules:
  0.0 187.9 jit_solution(14378576607472578759)
XLA Ops:
  7.2 0.8 fusion.40
  8.2 1.0 fusion.51
  9.2 1.3 convolution_convert_fusion.4
  11.6 16.4 %all-to-all-start = ((bf16[16,8,1280]{2,1,0:T(8,128)(2,1)}), bf16[16,8,1280]{2,1,0:T(8,128)(2,1)S(1)}, u32[]{:S(2)}, u32[]{:S(2)}) async-start(bf16[16,8,1280]{2,1,0:T(8,128)(2,1)} %maximum_bitcast_fusion), calls=%async_computation | async-start | bytes 655360 | tf_op jit(solution)/shard_map/all_to_all | solution.py:53
  28.7 0.8 maximum_bitcast_fusion.1
  29.5 9.3 %all-to-all-done = bf16[16,8,1280]{2,1,0:T(8,128)(2,1)S(1)} async-done(((bf16[16,8,1280]{2,1,0:T(8,128)(2,1)}), bf16[16,8,1280]{2,1,0:T(8,128)(2,1)S(1)}, u32[]{:S(2)}, u32[]{:S(2)}) %all-to-all-start) | async-done | bytes 327712 | tf_op jit(solution)/shard_map/all_to_all | solution.py:53
  38.8 5.3 %all-to-all-start.1 = ((bf16[16,8,1280]{2,1,0:T(8,128)(2,1)}), bf16[16,8,1280]{2,1,0:T(8,128)(2,1)S(1)}, u32[]{:S(2)}, u32[]{:S(2)}) async-start(bf16[16,8,1280]{2,1,0:T(8,128)(2,1)} %maximum_bitcast_fusion.1), calls=%async_computation.1 | async-start | bytes 655360 | tf_op jit(solution)/shard_map/all_to_all | solution.py:56
  44.2 0.8 pad_maximum_fusion.5
  45.0 9.9 %all-to-all-done.1 = bf16[16,8,1280]{2,1,0:T(8,128)(2,1)S(1)} async-done(((bf16[16,8,1280]{2,1,0:T(8,128)(2,1)}), bf16[16,8,1280]{2,1,0:T(8,128)(2,1)S(1)}, u32[]{:S(2)}, u32[]{:S(2)}) %all-to-all-start.1) | async-done | bytes 327712 | tf_op jit(solution)/shard_map/all_to_all | solution.py:56
  55.2 27.5 %all_to_all.25 = bf16[4,160,1024]{2,1,0:T(8,128)(2,1)S(1)} all-to-all(bf16[4,160,1024]{2,1,0:T(8,128)(2,1)S(1)} %broadcast_in_dim.18), channel_id=1, replica_groups=mesh['dp'=16,'fsdp'=4,'expert'=16] {'fsdp'}, dimensions={0} | all-to-all | bytes 2621440 | tf_op jit(solution)/shard_map/all_to_all | solution.py:60
  82.8 1.0 slice_bitcast_fusion.7
  83.8 3.1 %all-gather.2.cloned.1.call-done = bf16[160,4096]{1,0:T(8,128)(2,1)} async-done(((bf16[160,1024]{1,0:T(8,128)(2,1)}), bf16[160,4096]{1,0:T(8,128)(2,1)}) %all-gather.2.cloned.1.call-update) | async-done | bytes 1310736 | tf_op jit(solution)/shard_map/all_gather | solution.py:57
  86.8 2.1 %fusion.3 = f32[160,192]{1,0:T(8,128)S(1)} fusion(bf16[160,4096]{1,0:T(8,128)(2,1)} %all-gather.2.cloned.1.call-done, bf16[1,4096,192]{1,2,0:T(8,128)(2,1)S(1)} %copy-done), kind=kOutput, calls=%fused_computation.7 | convolution fusion | flops 251658240 | bytes 3006464 | tf_op jit(solution)/shard_map/dot_general | solution.py:72
  90.7 0.8 copy-done.13
  92.2 1.1 convolution_convert_fusion
  93.3 2.6 %pad_maximum_fusion = bf16[576,4096]{1,0:T(8,128)(2,1)} fusion(bf16[192,4096]{1,0:T(8,128)(2,1)S(1)} %convolution_convert_fusion.1, bf16[384,4096]{1,0:T(8,128)(2,1)S(1)} %convolution_convert_fusion), kind=kLoop, calls=%fused_computation.4 | loop fusion | flops 9437184 | bytes 9437184 | tf_op jit(solution)/shard_map/concatenate | solution.py:86
  96.0 0.9 copy-done.7
  98.2 20.6 %all_to_all.26 = bf16[4,160,1024]{2,1,0:T(8,128)(2,1)S(1)} all-to-all(bf16[4,160,1024]{2,1,0:T(8,128)(2,1)S(1)} %pad_maximum_fusion.2), channel_id=1, replica_groups=mesh['dp'=16,'fsdp'=4,'expert'=16] {'fsdp'}, dimensions={0} | all-to-all | bytes 2621440 | tf_op jit(solution)/shard_map/all_to_all | solution.py:96
  119.1 0.9 pad_maximum_fusion.3
  120.0 5.9 %all-to-all-start.4 = ((bf16[16,10,1024]{2,1,0:T(8,128)(2,1)}), bf16[16,10,1024]{2,1,0:T(8,128)(2,1)S(1)}, u32[]{:S(2)}, u32[]{:S(2)}) async-start(bf16[16,10,1024]{2,1,0:T(8,128)(2,1)} %pad_maximum_fusion.3), calls=%async_computation.4 | async-start | bytes 1048576 | tf_op jit(solution)/shard_map/all_to_all | solution.py:104
  125.9 14.2 %all-to-all-done.4 = bf16[16,10,1024]{2,1,0:T(8,128)(2,1)S(1)} async-done(((bf16[16,10,1024]{2,1,0:T(8,128)(2,1)}), bf16[16,10,1024]{2,1,0:T(8,128)(2,1)S(1)}, u32[]{:S(2)}, u32[]{:S(2)}) %all-to-all-start.4) | async-done | bytes 327712 | tf_op jit(solution)/shard_map/all_to_all | solution.py:104
  140.2 1.0 convolution_convert_fusion.2
  141.2 38.2 %reduce-scatter.2.cloned.1.call-done = bf16[576,256]{1,0:T(8,128)(2,1)} async-done(((bf16[576,4096]{1,0:T(8,128)(2,1)}), bf16[576,256]{1,0:T(8,128)(2,1)}) %reduce-scatter.2.cloned.1.call-update) | async-done | bytes 294928 | tf_op jit(solution)/shard_map/reduce_scatter | solution.py:89
  179.4 1.7 slice_bitcast_fusion.11
  (69 shorter events, 6.6 us)
Async XLA Ops:
  7.2 79.7 %copy-start = (bf16[1,4096,192]{1,2,0:T(8,128)(2,1)S(1)}, bf16[1,4096,192]{1,2,0:T(8,128)(2,1)}, u32[]{:S(2)}) copy-start(bf16[1,4096,192]{1,2,0:T(8,128)(2,1)} %param.11) | copy-start | bytes 4718596
  8.0 20.4 %copy-start.10 = (s32[128]{0:T(128)}, s32[128]{0:T(128)S(1)}, u32[]{:S(2)}) copy-start(s32[128]{0:T(128)S(1)} %fusion.40) | copy-start | bytes 1540
  8.2 1.0 copy-start.14
  9.2 18.9 %copy-start.9 = (s32[128,8]{0,1:T(8,128)S(1)}, s32[128,8]{0,1:T(8,128)}, u32[]{:S(2)}) copy-start(s32[128,8]{0,1:T(8,128)} %param.9) | copy-start | bytes 12292
  9.2 18.8 %copy-start.12 = (f32[128,8]{0,1:T(8,128)S(1)}, f32[128,8]{0,1:T(8,128)}, u32[]{:S(2)}) copy-start(f32[128,8]{0,1:T(8,128)} %param.10) | copy-start | bytes 12292
  9.2 18.9 %copy-start.8 = (bf16[128,1024]{1,0:T(8,128)(2,1)S(1)}, bf16[128,1024]{1,0:T(8,128)(2,1)}, u32[]{:S(2)}) copy-start(bf16[128,1024]{1,0:T(8,128)(2,1)} %param.8) | copy-start | bytes 786436
  11.6 27.2 %all-to-all-start = ((bf16[16,8,1280]{2,1,0:T(8,128)(2,1)}), bf16[16,8,1280]{2,1,0:T(8,128)(2,1)S(1)}, u32[]{:S(2)}, u32[]{:S(2)}) async-start(bf16[16,8,1280]{2,1,0:T(8,128)(2,1)} %maximum_bitcast_fusion), calls=%async_computation | async-start | bytes 655360 | tf_op jit(solution)/shard_map/all_to_all | solution.py:53
  38.8 16.2 %all-to-all-start.1 = ((bf16[16,8,1280]{2,1,0:T(8,128)(2,1)}), bf16[16,8,1280]{2,1,0:T(8,128)(2,1)S(1)}, u32[]{:S(2)}, u32[]{:S(2)}) async-start(bf16[16,8,1280]{2,1,0:T(8,128)(2,1)} %maximum_bitcast_fusion.1), calls=%async_computation.1 | async-start | bytes 655360 | tf_op jit(solution)/shard_map/all_to_all | solution.py:56
  44.1 42.8 %all-gather.2.cloned.1.call-start = ((), (), s32[]{:S(2)}) async-start(), calls=%async_computation.6 | async-start | bytes 1638400 | tf_op jit(solution)/shard_map/all_gather | solution.py:57
  45.0 134.4 %reduce-scatter.2.cloned.1.call-start = ((), (), s32[]{:S(2)}) async-start(), calls=%async_computation.7 | async-start | bytes 5013504 | tf_op jit(solution)/shard_map/reduce_scatter | solution.py:89
  83.8 5.2 %copy-start.2 = (bf16[1,4096,192]{1,2,0:T(8,128)(2,1)S(1)}, bf16[1,4096,192]{1,2,0:T(8,128)(2,1)}, u32[]{:S(2)}) copy-start(bf16[1,4096,192]{1,2,0:T(8,128)(2,1)} %param.12) | copy-start | bytes 4718596
  86.8 2.1 %copy-start.1 = (bf16[160,4096]{1,0:T(8,128)(2,1)S(1)}, bf16[160,4096]{1,0:T(8,128)(2,1)}, u32[]{:S(2)}) copy-start(bf16[160,4096]{1,0:T(8,128)(2,1)} %all-gather.2.cloned.1.call-done) | copy-start | bytes 3932164
  88.9 1.0 copy-start.3
  89.0 1.1 copy-start.4
  89.0 1.2 copy-start.5
  90.1 1.4 copy-start.13
  92.2 1.1 copy-start.6
  95.9 0.9 copy-start.7
  119.0 6.9 %copy-start.11 = (s32[128]{0:T(128)S(1)}, s32[128]{0:T(128)}, u32[]{:S(2)}) copy-start(s32[128]{0:T(128)} %copy-done.10) | copy-start | bytes 1540
  119.0 6.9 %copy-start.15 = (f32[128]{0:T(128)S(1)}, f32[128]{0:T(128)}, u32[]{:S(2)}) copy-start(f32[128]{0:T(128)} %copy-done.14) | copy-start | bytes 1540
  120.0 20.1 %all-to-all-start.4 = ((bf16[16,10,1024]{2,1,0:T(8,128)(2,1)}), bf16[16,10,1024]{2,1,0:T(8,128)(2,1)S(1)}, u32[]{:S(2)}, u32[]{:S(2)}) async-start(bf16[16,10,1024]{2,1,0:T(8,128)(2,1)} %pad_maximum_fusion.3), calls=%async_computation.4 | async-start | bytes 1048576 | tf_op jit(solution)/shard_map/all_to_all | solution.py:104
Sparse Core Ops, SparseCore 0:
  47.5 39.2 all-gather.1
  96.1 83.2 reduce-scatter.1

commit v2 on v1

v2 whole, which is shorter than its diff:
```python
import jax
import jax.numpy as jnp
from jax import lax
from jax.experimental import pallas as pl
from jax.experimental.pallas import tpu as pltpu
from jax.sharding import PartitionSpec as P

CAP = 10
MAIN = 8
TAIL = CAP - MAIN
PIECES = MAIN // TAIL
F32 = jnp.float32
BF16 = jnp.bfloat16
NN = (((1,), (0,)), ((), ()))
NT = (((1,), (1,)), ((), ()))
TN = (((0,), (0,)), ((), ()))


def dot(a, b, dims=NN):
    return lax.dot_general(a, b, dims, preferred_element_type=F32)


def iota(shape, axis):
    return lax.broadcasted_iota(jnp.int32, shape, axis)


def places(routes, owners):
    count = routes.shape[1]
    target = jnp.sum(jnp.where(routes < owners, routes, 0), axis=0, keepdims=True)
    mine = iota((owners, count), 0) == target
    earlier = (iota((count, count), 0) < iota((count, count), 1)).astype(BF16)
    before = dot(mine.astype(BF16), earlier)
    rank = jnp.sum(jnp.where(mine, before, 0.0), axis=0, keepdims=True).astype(jnp.int32)
    return target, rank


def send_kernel(
    owners, routes_hbm, gates_hbm, tokens_hbm, cotangent_hbm, out_ref, slot_ref,
    routes_ref, gates_ref, tokens_ref, cotangent_ref, sems,
):
    fetches = [
        pltpu.make_async_copy(source, near, sems.at[i])
        for i, (source, near) in enumerate(
            (
                (routes_hbm, routes_ref),
                (gates_hbm, gates_ref),
                (cotangent_hbm, cotangent_ref),
                (tokens_hbm, tokens_ref),
            )
        )
    ]
    for fetch in fetches:
        fetch.start()
    fetches[0].wait()
    routes = routes_ref[...]
    target, rank = places(routes, owners)
    slot_ref[...] = jnp.broadcast_to(target * CAP + rank, slot_ref.shape)
    fetches[1].wait()
    gate = jnp.where(routes < owners, gates_ref[...], 0.0)
    gate = jnp.sum(jnp.transpose(gate), axis=1, keepdims=True)
    fetches[2].wait()
    scaled = (gate * cotangent_ref[...].astype(F32)).astype(BF16)
    fetches[3].wait()
    values = jnp.concatenate([tokens_ref[...], scaled], axis=0)
    count, quarter = values.shape
    width = quarter // PIECES
    rows = owners * 2 * MAIN
    row, column = iota((rows, count), 0), iota((rows, count), 1)
    target = jnp.concatenate([target, target], axis=1)
    rank = jnp.concatenate([rank, rank], axis=1)
    place = row % MAIN
    wanted = (row // (2 * MAIN) == target) & (row // MAIN % 2 == column // (count // 2))
    main_pick = (wanted & (place == rank)).astype(BF16)
    out_ref[:, :quarter] = dot(main_pick, values).astype(BF16)
    in_tail = wanted & (place // PIECES + MAIN == rank)
    tail = jnp.zeros((rows, width), F32)
    for p in range(PIECES):
        pick = (in_tail & (place % PIECES == p)).astype(BF16)
        tail = tail + dot(pick, values[:, p * width : (p + 1) * width])
    out_ref[:, quarter:] = tail.astype(BF16)


def tail_pick(rows, p):
    tails = rows // MAIN * TAIL
    slot, row = iota((tails, rows), 0), iota((tails, rows), 1)
    return (row == slot // TAIL * MAIN + slot % TAIL * PIECES + p).astype(BF16)


def forward_kernel(rows_ref, gate_ref, up_ref, full_hbm, mid_hbm, full_ref, mid_ref, sems):
    quarters, mains, _ = rows_ref.shape
    quarter = full_ref.shape[1] // quarters
    width = quarter // PIECES
    wide = gate_ref.shape[0]
    picks = [tail_pick(mains, p) for p in range(PIECES)]
    for j in range(quarters):
        low = j * quarter
        full_ref[:mains, low : low + quarter] = rows_ref[j, :, :quarter]
        packed = rows_ref[j, :, quarter:]
        for p in range(PIECES):
            start = low + p * width
            full_ref[mains:, start : start + width] = dot(picks[p], packed).astype(BF16)
    keep_full = pltpu.make_async_copy(full_ref, full_hbm, sems.at[0])
    keep_full.start()
    gate_pre = jnp.zeros((wide, full_ref.shape[0]), F32)
    up_pre = jnp.zeros((wide, full_ref.shape[0]), F32)
    for j in range(quarters):
        low = j * quarter
        block = full_ref[:, low : low + quarter]
        gate_pre = gate_pre + dot(gate_ref[:, low : low + quarter], block, NT)
        up_pre = up_pre + dot(up_ref[:, low : low + quarter], block, NT)
    sigmoid_gate = jax.nn.sigmoid(gate_pre)
    activated = gate_pre * sigmoid_gate
    mid_ref[:wide, :] = up_pre * sigmoid_gate * (1.0 + gate_pre * (1.0 - sigmoid_gate))
    mid_ref[wide : 2 * wide, :] = activated
    mid_ref[2 * wide :, :] = activated * up_pre
    keep_mid = pltpu.make_async_copy(mid_ref, mid_hbm, sems.at[1])
    keep_mid.start()
    keep_full.wait()
    keep_mid.wait()


def backward_kernel(
    grads_hbm, down_hbm, full_hbm, mid_hbm, terms_hbm, pair_hbm,
    grads_ref, down_ref, full_ref, mid_ref, pair_ref, block_ref, tails_ref, sems,
):
    quarters, mains, _ = grads_ref.shape
    quarter = full_ref.shape[1] // quarters
    width = quarter // PIECES
    wide = down_ref.shape[0]

    def columns(ref, j):
        return ref.at[:, j * quarter : (j + 1) * quarter]

    grads_in = [
        pltpu.make_async_copy(grads_hbm.at[j], grads_ref.at[j], sems.at[0, j])
        for j in range(quarters)
    ]
    down_in = [
        pltpu.make_async_copy(columns(down_hbm, j), columns(down_ref, j), sems.at[1, j])
        for j in range(quarters)
    ]
    full_in = [
        pltpu.make_async_copy(columns(full_hbm, j), columns(full_ref, j), sems.at[2, j])
        for j in range(quarters)
    ]
    mid_in = pltpu.make_async_copy(mid_hbm, mid_ref, sems.at[4, 0])
    for j in range(quarters):
        grads_in[j].start()
        down_in[j].start()
    mid_in.start()
    for j in range(quarters):
        full_in[j].start()
    picks = [tail_pick(mains, p) for p in range(PIECES)]
    main_grad = jnp.zeros((wide, mains), F32)
    tail_grad = jnp.zeros((wide, full_ref.shape[0] - mains), F32)
    for j in range(quarters):
        low = j * quarter
        grads_in[j].wait()
        packed = grads_ref[j, :, quarter:]
        for p in range(PIECES):
            start = low + p * width
            tails_ref[:, start : start + width] = dot(picks[p], packed).astype(BF16)
        down_in[j].wait()
        weight = down_ref[:, low : low + quarter]
        main_grad = main_grad + dot(weight, grads_ref[j, :, :quarter], NT)
        tail_grad = tail_grad + dot(weight, tails_ref[:, low : low + quarter], NT)
    hidden_grad = jnp.concatenate([main_grad, tail_grad], axis=1)
    mid_in.wait()
    pair_ref[:wide, :] = (hidden_grad * mid_ref[:wide, :]).astype(BF16)
    pair_ref[wide:, :] = (hidden_grad * mid_ref[wide : 2 * wide, :]).astype(BF16)
    hidden = mid_ref[2 * wide :, :].astype(BF16)
    outs = [pltpu.make_async_copy(pair_ref, pair_hbm, sems.at[4, 1])]
    outs[0].start()
    for j in range(quarters):
        low = j * quarter
        full_in[j].wait()
        block_ref[j, : 2 * wide, :] = dot(
            pair_ref[...], full_ref[:, low : low + quarter]
        ).astype(BF16)
        down_term = dot(hidden[:, :mains], grads_ref[j, :, :quarter])
        down_term = down_term + dot(hidden[:, mains:], tails_ref[:, low : low + quarter])
        block_ref[j, 2 * wide :, :] = down_term.astype(BF16)
        out = pltpu.make_async_copy(block_ref.at[j], columns(terms_hbm, j), sems.at[3, j])
        out.start()
        outs.append(out)
    for out in outs:
        out.wait()


def vmem():
    return pl.BlockSpec(memory_space=pltpu.VMEM)


def hbm():
    return pl.BlockSpec(memory_space=pltpu.HBM)


def far(*arrays):
    return [pltpu.with_memory_space_constraint(x, pltpu.HBM) for x in arrays]


def call(kernel, operands, outs, name, limit_mib, in_specs=None, out_specs=None, scratch=()):
    return pl.pallas_call(
        kernel,
        out_shape=outs,
        in_specs=in_specs if in_specs is not None else [vmem() for _ in operands],
        out_specs=out_specs if out_specs is not None else [vmem() for _ in outs],
        scratch_shapes=scratch,
        compiler_params=pltpu.CompilerParams(vmem_limit_bytes=limit_mib * 1024 * 1024),
        name=name,
    )(*operands)


def local(tokens, cotangent, routes, route_gates, gate_weight, up_weight, down_weight):
    owners = lax.axis_size("expert")
    quarters = lax.axis_size("fsdp")
    count, quarter = tokens.shape
    model = quarter * quarters
    mains = owners * MAIN
    slots = owners * CAP
    packed_width = quarter + quarter // PIECES

    def to_owners(x):
        return lax.all_to_all(x, "expert", split_axis=0, concat_axis=0, tiled=True)

    def to_quarters(x):
        return lax.all_to_all(x, "fsdp", split_axis=0, concat_axis=0, tiled=True)

    sent, slot = call(
        lambda *refs: send_kernel(owners, *refs),
        far(routes.T, route_gates.T, tokens, cotangent),
        (
            jax.ShapeDtypeStruct((2 * mains, packed_width), BF16),
            jax.ShapeDtypeStruct((8, count), jnp.int32),
        ),
        "send",
        8,
        in_specs=[hbm()] * 4,
        scratch=[
            pltpu.VMEM(routes.shape[::-1], jnp.int32),
            pltpu.VMEM(route_gates.shape[::-1], F32),
            pltpu.VMEM(tokens.shape, BF16),
            pltpu.VMEM(cotangent.shape, BF16),
            pltpu.SemaphoreType.DMA((4,)),
        ],
    )
    received = to_owners(sent.reshape(owners, 2 * MAIN, packed_width))
    recv_rows = received[:, :MAIN].reshape(mains, packed_width)
    recv_grads = received[:, MAIN:].reshape(mains, packed_width)
    grads4 = lax.all_gather(recv_grads, "fsdp", axis=0, tiled=True)
    grads4 = grads4.reshape(quarters, mains, packed_width)
    rows4 = to_quarters(jnp.broadcast_to(recv_rows[None], (quarters, mains, packed_width)))
    gate_mat = jnp.swapaxes(gate_weight, 1, 2)[0]
    up_mat = jnp.swapaxes(up_weight, 1, 2)[0]
    down_mat = down_weight[0]
    width = gate_mat.shape[0]
    full_rows, mid = call(
        forward_kernel,
        (rows4, gate_mat, up_mat),
        (pltpu.HBM((slots, model), BF16), pltpu.HBM((3 * width, slots), F32)),
        "forward",
        12,
        out_specs=[hbm(), hbm()],
        scratch=[
            pltpu.VMEM((slots, model), BF16),
            pltpu.VMEM((3 * width, slots), F32),
            pltpu.SemaphoreType.DMA((2,)),
        ],
    )
    terms, pair = call(
        backward_kernel,
        far(grads4, down_mat, full_rows, mid),
        (pltpu.HBM((3 * width, model), BF16), pltpu.HBM((2 * width, slots), BF16)),
        "backward",
        16,
        in_specs=[hbm()] * 4,
        out_specs=[hbm(), hbm()],
        scratch=[
            pltpu.VMEM((quarters, mains, packed_width), BF16),
            pltpu.VMEM((width, model), BF16),
            pltpu.VMEM((slots, model), BF16),
            pltpu.VMEM((3 * width, slots), F32),
            pltpu.VMEM((2 * width, slots), BF16),
            pltpu.VMEM((quarters, 3 * width, quarter), BF16),
            pltpu.VMEM((slots - mains, model), BF16),
            pltpu.SemaphoreType.DMA((5, quarters)),
        ],
    )
    sums = lax.psum_scatter(terms, "dp", scatter_dimension=1, tiled=True)
    partial_value = dot(pair[:width], gate_mat, TN) + dot(pair[width:], up_mat, TN)
    blocks = partial_value.astype(BF16)
    blocks = jnp.stack([blocks[:, k * quarter : (k + 1) * quarter] for k in range(quarters)])
    given = to_quarters(blocks).astype(F32)
    route_rows = (given[0] + given[1] + given[2] + given[3]).astype(BF16)
    returned = to_owners(
        jnp.concatenate(
            [
                route_rows[:mains].reshape(owners, MAIN, quarter),
                route_rows[mains:].reshape(owners, TAIL, quarter),
            ],
            axis=1,
        )
    )
    selector = (jnp.arange(slots, dtype=jnp.int32)[:, None] == slot[:1]).astype(BF16)
    token_grads = dot(selector, returned.reshape(slots, quarter), TN).astype(BF16)
    return (
        token_grads,
        sums[:width].T[None],
        sums[width : 2 * width].T[None],
        sums[2 * width :][None],
    )


def solution(mesh):
    placed = (
        P(("dp", "expert"), "fsdp"),
        P(("dp", "expert"), "fsdp"),
        P(("dp", "expert"), None),
        P(("dp", "expert"), None),
        P("expert", None, "fsdp"),
        P("expert", None, "fsdp"),
        P("expert", "fsdp", None),
    )
    return jax.shard_map(
        local,
        mesh=mesh,
        in_specs=placed,
        out_specs=(
            P(("dp", "expert"), "fsdp"),
            P("expert", "dp", "fsdp"),
            P("expert", "dp", "fsdp"),
            P("expert", "fsdp", "dp"),
        ),
        check_vma=False,
    )
```

time: 189 us -> 178 us (0.942)
  the two profiles are of different devices: /device:TPU:8 before, /device:TPU:2 now
where the time goes in v2:
time: 178 us
  blocking collectives  78.5 us (44%)
  waiting for transfers between devices  63.3 us (36%)
  between operations  14.2 us (8%)
  Pallas kernels  10.1 us (6%)
  starting transfers between devices  4.42 us (2%)
  local copies, waits for them, and re-layouts  3.75 us (2%)
  matrix products  2.09 us (1%)
    all_to_all x2, blocking collectives, to_quarters(): return lax.all_to_all(x, 'fsdp', split_axis=0, concat_axis=0, tiled=True)  51.5 us
    reduce_scatter x1, waiting for transfers between devices, local(): sums = lax.psum_scatter(terms, 'dp', scatter_dimension=1, tiled=True)  40.6 us
    all_to_all x1, blocking collectives, to_owners(): return lax.all_to_all(x, 'expert', split_axis=0, concat_axis=0, tiled=True)  27 us
    all_to_all x1, waiting for transfers between devices, to_owners(): return lax.all_to_all(x, 'expert', split_axis=0, concat_axis=0, tiled=True)  15.9 us
    pallas_call x3, Pallas kernels, call(): pl.pallas_call(kernel, out_shape=outs, in_specs=in_specs if in_specs is n...  10.1 us
    all_gather x1, waiting for transfers between devices, local(): grads4 = lax.all_gather(recv_grads, 'fsdp', axis=0, tiled=True)  6.77 us
    all_to_all x1, starting transfers between devices, to_owners(): return lax.all_to_all(x, 'expert', split_axis=0, concat_axis=0, tiled=True)  4.34 us
  transfers between devices with their start and end apart: 3, of which 3 were waited for; matrix products, arithmetic and copies ran while one was open for 2% of the time, Pallas kernels for 1%

profile of v2, /device:TPU:2, one launch (start us, length us, event | category | flops | bytes accessed | tf_op | source)
XLA Modules:
  0.0 177.9 jit_solution(97703111435940198)
XLA Ops:
  7.2 1.6 send.1
  8.8 27.0 %all_to_all.20 = bf16[16,16,1280]{2,1,0:T(8,128)(2,1)S(1)} all-to-all(bf16[16,16,1280]{2,1,0:T(8,128)(2,1)S(1)} %bitcast.44), channel_id=1, replica_groups=mesh['dp'=16,'fsdp'=4,'expert'=16] {'expert'}, dimensions={0} | all-to-all | bytes 1310720 | tf_op jit(solution)/shard_map/all_to_all | solution.py:224
  35.8 0.8 slice_bitcast_fusion.4
  36.6 0.0 reduce-scatter.2.cloned.1.call-start
  36.6 0.1 broadcast_in_dim.18
  36.7 31.0 %all_to_all.21.rows_ref = bf16[4,128,1280]{2,1,0:T(8,128)(2,1)S(1)} all-to-all(bf16[4,128,1280]{2,1,0:T(8,128)(2,1)S(1)} %broadcast_in_dim.18), channel_id=1, replica_groups=mesh['dp'=16,'fsdp'=4,'expert'=16] {'fsdp'}, dimensions={0} | all-to-all | bytes 2621440 | tf_op jit(solution)/shard_map/all_to_all | solution.py:227
  67.8 2.3 %forward.1 = (bf16[160,4096]{1,0:T(8,128)(2,1)}, f32[576,160]{1,0:T(8,128)}) custom-call(bf16[4,128,1280]{2,1,0:T(8,128)(2,1)S(1)} %all_to_all.21.rows_ref, bf16[192,4096]{1,0:T(8,128)(2,1)S(1)} %bitcast.42, bf16[192,4096]{1,0:T(8,128)(2,1)S(1)} %bitcast.43), custom_call_target="tpu_custom_call" | custom-call | tf_op jit(solution)/shard_map/forward/pallas_call | solution.py:203
  70.0 6.8 %all-gather.2.cloned.1.call-done = bf16[512,1280]{1,0:T(8,128)(2,1)} async-done(((bf16[128,1280]{1,0:T(8,128)(2,1)}), bf16[512,1280]{1,0:T(8,128)(2,1)}) %all-gather.2.cloned.1.call-update) | async-done | bytes 1310736 | tf_op jit(solution)/shard_map/all_gather | solution.py:250
  76.8 6.2 %backward.1 = (bf16[576,4096]{1,0:T(8,128)(2,1)}, bf16[384,160]{1,0:T(8,128)(2,1)}) custom-call(bf16[4,128,1280]{2,1,0:T(8,128)(2,1)} %bitcast.46, bf16[192,4096]{1,0:T(8,128)(2,1)} %bitcast.45, bf16[160,4096]{1,0:T(8,128)(2,1)} %get-tuple-element.12.full_hbm, f32[576,160]{1,0:T(8,128)} %get-tuple-element.13.mid_hbm), custom_call_target="tpu_custom_call" | custom-call | tf_op jit(solution)/shard_map/backward/pallas_call | solution.py:203
  83.1 0.9 copy-done.2
  84.0 0.5 fusion.3
  84.5 0.6 fusion
  85.1 0.1 slice_bitcast_fusion.3
  85.2 0.2 pad_maximum_fusion
  85.4 20.5 %all_to_all.22 = bf16[4,160,1024]{2,1,0:T(8,128)(2,1)S(1)} all-to-all(bf16[4,160,1024]{2,1,0:T(8,128)(2,1)S(1)} %pad_maximum_fusion), channel_id=1, replica_groups=mesh['dp'=16,'fsdp'=4,'expert'=16] {'fsdp'}, dimensions={0} | all-to-all | bytes 2621440 | tf_op jit(solution)/shard_map/all_to_all | solution.py:227
  105.9 0.3 convert_element_type.15
  106.2 0.2 fusion.1
  106.4 0.9 pad_maximum_fusion.1
  107.3 4.3 %all-to-all-start.3 = ((bf16[16,10,1024]{2,1,0:T(8,128)(2,1)}), bf16[16,10,1024]{2,1,0:T(8,128)(2,1)S(1)}, u32[]{:S(2)}, u32[]{:S(2)}) async-start(bf16[16,10,1024]{2,1,0:T(8,128)(2,1)} %pad_maximum_fusion.1), calls=%async_computation.3 | async-start | bytes 1048576 | tf_op jit(solution)/shard_map/all_to_all | solution.py:224
  111.7 15.9 %all-to-all-done.3 = bf16[16,10,1024]{2,1,0:T(8,128)(2,1)S(1)} async-done(((bf16[16,10,1024]{2,1,0:T(8,128)(2,1)}), bf16[16,10,1024]{2,1,0:T(8,128)(2,1)S(1)}, u32[]{:S(2)}, u32[]{:S(2)}) %all-to-all-start.3) | async-done | bytes 327712 | tf_op jit(solution)/shard_map/all_to_all | solution.py:224
  127.6 0.1 reshape.40
  127.7 1.0 convolution_convert_fusion
  128.7 40.6 %reduce-scatter.2.cloned.1.call-done = bf16[576,256]{1,0:T(8,128)(2,1)} async-done(((bf16[576,4096]{1,0:T(8,128)(2,1)}), bf16[576,256]{1,0:T(8,128)(2,1)}) %reduce-scatter.2.cloned.1.call-update) | async-done | bytes 294928 | tf_op jit(solution)/shard_map/reduce_scatter | solution.py:289
  169.3 1.7 slice_bitcast_fusion.7
  (12 shorter events, 0.1 us)
Async XLA Ops:
  7.2 69.6 %all-gather.2.cloned.1.call-start = ((), (), s32[]{:S(2)}) async-start(), calls=%async_computation.5 | async-start | bytes 1638400 | tf_op jit(solution)/shard_map/all_gather | solution.py:250
  36.6 132.8 %reduce-scatter.2.cloned.1.call-start = ((), (), s32[]{:S(2)}) async-start(), calls=%async_computation.6 | async-start | bytes 5013504 | tf_op jit(solution)/shard_map/reduce_scatter | solution.py:289
  36.6 31.2 %copy-start.1 = (bf16[1,4096,192]{1,2,0:T(8,128)(2,1)S(1)}, bf16[1,4096,192]{1,2,0:T(8,128)(2,1)}, u32[]{:S(2)}) copy-start(bf16[1,4096,192]{1,2,0:T(8,128)(2,1)} %param.12) | copy-start | bytes 4718596
  36.7 31.1 %copy-start = (bf16[1,4096,192]{1,2,0:T(8,128)(2,1)S(1)}, bf16[1,4096,192]{1,2,0:T(8,128)(2,1)}, u32[]{:S(2)}) copy-start(bf16[1,4096,192]{1,2,0:T(8,128)(2,1)} %param.11) | copy-start | bytes 4718596
  83.0 0.9 copy-start.2
  107.3 20.3 %all-to-all-start.3 = ((bf16[16,10,1024]{2,1,0:T(8,128)(2,1)}), bf16[16,10,1024]{2,1,0:T(8,128)(2,1)S(1)}, u32[]{:S(2)}, u32[]{:S(2)}) async-start(bf16[16,10,1024]{2,1,0:T(8,128)(2,1)} %pad_maximum_fusion.1), calls=%async_computation.3 | async-start | bytes 1048576 | tf_op jit(solution)/shard_map/all_to_all | solution.py:224
Sparse Core Ops, SparseCore 0:
  36.7 40.0 all-gather.1
  83.2 86.0 reduce-scatter.1

commit v3 on v2

--- a/solution.py
+++ b/solution.py
@@ -8,6 +8,7 @@
 CAP = 10
 MAIN = 8
 TAIL = CAP - MAIN
+LATE = 16
 PIECES = MAIN // TAIL
 F32 = jnp.float32
 BF16 = jnp.bfloat16
@@ -86,21 +87,32 @@
     return (row == slot // TAIL * MAIN + slot % TAIL * PIECES + p).astype(BF16)
 
 
-def forward_kernel(rows_ref, gate_ref, up_ref, full_hbm, mid_hbm, full_ref, mid_ref, sems):
-    quarters, mains, _ = rows_ref.shape
+def forward_kernel(
+    rows_ref, gate_ref, up_ref, full_hbm, mid_hbm, late_hbm, late_tail_hbm,
+    full_ref, mid_ref, late_ref, late_tail_ref, sems,
+):
+    quarters, both, _ = rows_ref.shape
+    mains = both - LATE
     quarter = full_ref.shape[1] // quarters
     width = quarter // PIECES
     wide = gate_ref.shape[0]
     picks = [tail_pick(mains, p) for p in range(PIECES)]
     for j in range(quarters):
         low = j * quarter
-        full_ref[:mains, low : low + quarter] = rows_ref[j, :, :quarter]
-        packed = rows_ref[j, :, quarter:]
+        full_ref[:mains, low : low + quarter] = rows_ref[j, :mains, :quarter]
+        packed = rows_ref[j, :mains, quarter:]
         for p in range(PIECES):
             start = low + p * width
             full_ref[mains:, start : start + width] = dot(picks[p], packed).astype(BF16)
-    keep_full = pltpu.make_async_copy(full_ref, full_hbm, sems.at[0])
-    keep_full.start()
+        late_ref[:, low : low + quarter] = rows_ref[j, mains:, :quarter]
+        late_tail_ref[j] = rows_ref[j, mains:, quarter:]
+    keeps = [
+        pltpu.make_async_copy(full_ref, full_hbm, sems.at[0]),
+        pltpu.make_async_copy(late_ref, late_hbm, sems.at[1]),
+        pltpu.make_async_copy(late_tail_ref, late_tail_hbm, sems.at[2]),
+    ]
+    for keep in keeps:
+        keep.start()
     gate_pre = jnp.zeros((wide, full_ref.shape[0]), F32)
     up_pre = jnp.zeros((wide, full_ref.shape[0]), F32)
     for j in range(quarters):
@@ -113,17 +125,18 @@
     mid_ref[:wide, :] = up_pre * sigmoid_gate * (1.0 + gate_pre * (1.0 - sigmoid_gate))
     mid_ref[wide : 2 * wide, :] = activated
     mid_ref[2 * wide :, :] = activated * up_pre
-    keep_mid = pltpu.make_async_copy(mid_ref, mid_hbm, sems.at[1])
-    keep_mid.start()
-    keep_full.wait()
-    keep_mid.wait()
+    keeps.append(pltpu.make_async_copy(mid_ref, mid_hbm, sems.at[3]))
+    keeps[3].start()
+    for keep in keeps:
+        keep.wait()
 
 
 def backward_kernel(
-    grads_hbm, down_hbm, full_hbm, mid_hbm, terms_hbm, pair_hbm,
-    grads_ref, down_ref, full_ref, mid_ref, pair_ref, block_ref, tails_ref, sems,
+    grads_hbm, late_hbm, late_tail_hbm, down_hbm, full_hbm, mid_hbm, terms_hbm, pair_hbm,
+    grads_ref, tail_ref, down_ref, full_ref, mid_ref, pair_ref, pairs_ref, downs_ref, sems,
 ):
-    quarters, mains, _ = grads_ref.shape
+    quarters, early, _ = grads_hbm.shape
+    mains = early + LATE
     quarter = full_ref.shape[1] // quarters
     width = quarter // PIECES
     wide = down_ref.shape[0]
@@ -131,8 +144,20 @@
     def columns(ref, j):
         return ref.at[:, j * quarter : (j + 1) * quarter]
 
+    mid_in = pltpu.make_async_copy(mid_hbm, mid_ref, sems.at[5, 0])
+    tail_in = pltpu.make_async_copy(
+        grads_hbm.at[:, :, quarter:], tail_ref.at[:, :early, :], sems.at[5, 1]
+    )
+    late_tail_in = pltpu.make_async_copy(
+        late_tail_hbm, tail_ref.at[:, early:, :], sems.at[5, 2]
+    )
+    late_in = pltpu.make_async_copy(late_hbm, grads_ref.at[early:mains, :], sems.at[5, 3])
     grads_in = [
-        pltpu.make_async_copy(grads_hbm.at[j], grads_ref.at[j], sems.at[0, j])
+        pltpu.make_async_copy(
+            grads_hbm.at[j, :, :quarter],
+            grads_ref.at[:early, j * quarter : (j + 1) * quarter],
+            sems.at[0, j],
+        )
         for j in range(quarters)
     ]
     down_in = [
@@ -143,48 +168,74 @@
         pltpu.make_async_copy(columns(full_hbm, j), columns(full_ref, j), sems.at[2, j])
         for j in range(quarters)
     ]
-    mid_in = pltpu.make_async_copy(mid_hbm, mid_ref, sems.at[4, 0])
-    for j in range(quarters):
+    tail_in.start()
+    late_tail_in.start()
+    late_in.start()
+    grads_in[0].start()
+    down_in[0].start()
+    mid_in.start()
+    for j in range(1, quarters):
         grads_in[j].start()
         down_in[j].start()
-    mid_in.start()
     for j in range(quarters):
         full_in[j].start()
     picks = [tail_pick(mains, p) for p in range(PIECES)]
-    main_grad = jnp.zeros((wide, mains), F32)
-    tail_grad = jnp.zeros((wide, full_ref.shape[0] - mains), F32)
+    hidden_grad = jnp.zeros((wide, grads_ref.shape[0]), F32)
+    tail_in.wait()
+    late_tail_in.wait()
+    late_in.wait()
+    outs = []
     for j in range(quarters):
         low = j * quarter
-        grads_in[j].wait()
-        packed = grads_ref[j, :, quarter:]
         for p in range(PIECES):
             start = low + p * width
-            tails_ref[:, start : start + width] = dot(picks[p], packed).astype(BF16)
+            grads_ref[mains:, start : start + width] = dot(picks[p], tail_ref[j]).astype(BF16)
+        grads_in[j].wait()
         down_in[j].wait()
-        weight = down_ref[:, low : low + quarter]
-        main_grad = main_grad + dot(weight, grads_ref[j, :, :quarter], NT)
-        tail_grad = tail_grad + dot(weight, tails_ref[:, low : low + quarter], NT)
-    hidden_grad = jnp.concatenate([main_grad, tail_grad], axis=1)
-    mid_in.wait()
+        block = grads_ref[:, low : low + quarter]
+        hidden_grad = hidden_grad + dot(down_ref[:, low : low + quarter], block, NT)
+        if j == 0:
+            mid_in.wait()
+            hidden = mid_ref[2 * wide :, :].astype(BF16)
+        downs_ref[j] = dot(hidden, block).astype(BF16)
+        out = pltpu.make_async_copy(
+            downs_ref.at[j],
+            terms_hbm.at[2 * wide :, low : low + quarter],
+            sems.at[3, j],
+        )
+        out.start()
+        outs.append(out)
     pair_ref[:wide, :] = (hidden_grad * mid_ref[:wide, :]).astype(BF16)
     pair_ref[wide:, :] = (hidden_grad * mid_ref[wide : 2 * wide, :]).astype(BF16)
-    hidden = mid_ref[2 * wide :, :].astype(BF16)
-    outs = [pltpu.make_async_copy(pair_ref, pair_hbm, sems.at[4, 1])]
-    outs[0].start()
+    out = pltpu.make_async_copy(pair_ref, pair_hbm, sems.at[6, 0])
+    out.start()
+    outs.append(out)
     for j in range(quarters):
         low = j * quarter
         full_in[j].wait()
-        block_ref[j, : 2 * wide, :] = dot(
-            pair_ref[...], full_ref[:, low : low + quarter]
-        ).astype(BF16)
-        down_term = dot(hidden[:, :mains], grads_ref[j, :, :quarter])
-        down_term = down_term + dot(hidden[:, mains:], tails_ref[:, low : low + quarter])
-        block_ref[j, 2 * wide :, :] = down_term.astype(BF16)
-        out = pltpu.make_async_copy(block_ref.at[j], columns(terms_hbm, j), sems.at[3, j])
+        pairs_ref[j] = dot(pair_ref[...], full_ref[:, low : low + quarter]).astype(BF16)
+        out = pltpu.make_async_copy(
+            pairs_ref.at[j],
+            terms_hbm.at[: 2 * wide, low : low + quarter],
+            sems.at[4, j],
+        )
         out.start()
         outs.append(out)
     for out in outs:
         out.wait()
+
+
+def split_kernel(sums_hbm, *refs):
+    sems = refs[-1]
+    wide = sums_hbm.shape[0] // (len(refs) - 1)
+    copies = [
+        pltpu.make_async_copy(sums_hbm.at[i * wide : (i + 1) * wide, :], part, sems.at[i])
+        for i, part in enumerate(refs[:-1])
+    ]
+    for copy in copies:
+        copy.start()
+    for copy in copies:
+        copy.wait()
 
 
 def vmem():
@@ -247,43 +298,54 @@
     received = to_owners(sent.reshape(owners, 2 * MAIN, packed_width))
     recv_rows = received[:, :MAIN].reshape(mains, packed_width)
     recv_grads = received[:, MAIN:].reshape(mains, packed_width)
-    grads4 = lax.all_gather(recv_grads, "fsdp", axis=0, tiled=True)
-    grads4 = grads4.reshape(quarters, mains, packed_width)
-    rows4 = to_quarters(jnp.broadcast_to(recv_rows[None], (quarters, mains, packed_width)))
+    early = mains - LATE
+    grads4 = lax.all_gather(recv_grads[:early], "fsdp", axis=0, tiled=True)
+    grads4 = grads4.reshape(quarters, early, packed_width)
+    near = jnp.concatenate([recv_rows, recv_grads[early:]], axis=0)
+    rows4 = to_quarters(jnp.broadcast_to(near[None], (quarters, mains + LATE, packed_width)))
     gate_mat = jnp.swapaxes(gate_weight, 1, 2)[0]
     up_mat = jnp.swapaxes(up_weight, 1, 2)[0]
     down_mat = down_weight[0]
     width = gate_mat.shape[0]
-    full_rows, mid = call(
+    tail_width = packed_width - quarter
+    full_rows, mid, late, late_tail = call(
         forward_kernel,
         (rows4, gate_mat, up_mat),
-        (pltpu.HBM((slots, model), BF16), pltpu.HBM((3 * width, slots), F32)),
+        (
+            pltpu.HBM((slots, model), BF16),
+            pltpu.HBM((3 * width, slots), F32),
+            pltpu.HBM((LATE, model), BF16),
+            pltpu.HBM((quarters, LATE, tail_width), BF16),
+        ),
         "forward",
         12,
+        out_specs=[hbm()] * 4,
+        scratch=[
+            pltpu.VMEM((slots, model), BF16),
+            pltpu.VMEM((3 * width, slots), F32),
+            pltpu.VMEM((LATE, model), BF16),
+            pltpu.VMEM((quarters, LATE, tail_width), BF16),
+            pltpu.SemaphoreType.DMA((4,)),
+        ],
+    )
+    terms, pair = call(
+        backward_kernel,
+        far(grads4, late, late_tail, down_mat, full_rows, mid),
+        (pltpu.HBM((3 * width, model), BF16), pltpu.HBM((2 * width, slots), BF16)),
+        "backward",
+        16,
+        in_specs=[hbm()] * 6,
         out_specs=[hbm(), hbm()],
         scratch=[
             pltpu.VMEM((slots, model), BF16),
-            pltpu.VMEM((3 * width, slots), F32),
-            pltpu.SemaphoreType.DMA((2,)),
-        ],
-    )
-    terms, pair = call(
-        backward_kernel,
-        far(grads4, down_mat, full_rows, mid),
-        (pltpu.HBM((3 * width, model), BF16), pltpu.HBM((2 * width, slots), BF16)),
-        "backward",
-        16,
-        in_specs=[hbm()] * 4,
-        out_specs=[hbm(), hbm()],
-        scratch=[
-            pltpu.VMEM((quarters, mains, packed_width), BF16),
+            pltpu.VMEM((quarters, mains, tail_width), BF16),
             pltpu.VMEM((width, model), BF16),
             pltpu.VMEM((slots, model), BF16),
             pltpu.VMEM((3 * width, slots), F32),
             pltpu.VMEM((2 * width, slots), BF16),
-            pltpu.VMEM((quarters, 3 * width, quarter), BF16),
-            pltpu.VMEM((slots - mains, model), BF16),
-            pltpu.SemaphoreType.DMA((5, quarters)),
+            pltpu.VMEM((quarters, 2 * width, quarter), BF16),
+            pltpu.VMEM((quarters, width, quarter), BF16),
+            pltpu.SemaphoreType.DMA((7, 4)),
         ],
     )
     sums = lax.psum_scatter(terms, "dp", scatter_dimension=1, tiled=True)
@@ -303,12 +365,18 @@
     )
     selector = (jnp.arange(slots, dtype=jnp.int32)[:, None] == slot[:1]).astype(BF16)
     token_grads = dot(selector, returned.reshape(slots, quarter), TN).astype(BF16)
-    return (
-        token_grads,
-        sums[:width].T[None],
-        sums[width : 2 * width].T[None],
-        sums[2 * width :][None],
-    )
+    piece = pltpu.HBM((width, sums.shape[1]), BF16)
+    gate_sum, up_sum, down_sum = call(
+        split_kernel,
+        far(sums),
+        (piece, piece, piece),
+        "split",
+        4,
+        in_specs=[hbm()],
+        out_specs=[hbm()] * 3,
+        scratch=[pltpu.SemaphoreType.DMA((3,))],
+    )
+    return token_grads, gate_sum.T[None], up_sum.T[None], down_sum[None]
 
 
 def solution(mesh):

time: 178 us -> 186 us (1.045)
  Pallas kernels: 10.1 us -> 19.6 us
  blocking collectives: 78.5 us -> 82.1 us
  waiting for transfers between devices: 63.3 us -> 59.9 us
    pallas_call x3 -> x4, Pallas kernels: 10.1 us -> 19.6 us  [call(): pl.pallas_call(kernel, out_shape=outs, in_specs=in_specs if in_specs is n...]
    all_to_all x2, blocking collectives: 51.5 us -> 55.2 us  [to_quarters(): return lax.all_to_all(x, 'fsdp', split_axis=0, concat_axis=0, tiled=True)]
    all_gather x1, waiting for transfers between devices: 6.77 us -> 3.82 us  [local(): grads4 = lax.all_gather(recv_grads[:early], 'fsdp', axis=0, tiled=True)]
    broadcast_in_dim x3 -> x1, local copies, waits for them, and re-layouts: 2.55 us -> 0.1 us  [local(): jnp.broadcast_to(near[None], (quarters, mains + LATE, packed_width))]
where the time goes in v3:
time: 186 us; the launch traced here: 185 us
  blocking collectives  82.1 us (44%)
  waiting for transfers between devices  59.9 us (32%)
  Pallas kernels  19.6 us (11%)
  between operations  14.2 us (8%)
  starting transfers between devices  3.65 us (2%)
  matrix products  2.08 us (1%)
  local copies, waits for them, and re-layouts  2.06 us (1%)
    all_to_all x2, blocking collectives, to_quarters(): return lax.all_to_all(x, 'fsdp', split_axis=0, concat_axis=0, tiled=True)  55.2 us
    reduce_scatter x1, waiting for transfers between devices, local(): sums = lax.psum_scatter(terms, 'dp', scatter_dimension=1, tiled=True)  40.2 us
    all_to_all x1, blocking collectives, to_owners(): return lax.all_to_all(x, 'expert', split_axis=0, concat_axis=0, tiled=True)  27 us
    pallas_call x4, Pallas kernels, call(): pl.pallas_call(kernel, out_shape=outs, in_specs=in_specs if in_specs is n...  19.6 us
    all_to_all x1, waiting for transfers between devices, to_owners(): return lax.all_to_all(x, 'expert', split_axis=0, concat_axis=0, tiled=True)  15.9 us
    all_gather x1, waiting for transfers between devices, local(): grads4 = lax.all_gather(recv_grads[:early], 'fsdp', axis=0, tiled=True)  3.82 us
  transfers between devices with their start and end apart: 3, of which 3 were waited for; matrix products, arithmetic and copies ran while one was open for 2% of the time, Pallas kernels for 1%

profile of v3, /device:TPU:2, one launch (start us, length us, event | category | flops | bytes accessed | tf_op | source)
XLA Modules:
  0.0 185.2 jit_solution(15721782717736182822)
XLA Ops:
  7.2 1.6 send.1
  8.8 27.0 %all_to_all.20 = bf16[16,16,1280]{2,1,0:T(8,128)(2,1)S(1)} all-to-all(bf16[16,16,1280]{2,1,0:T(8,128)(2,1)S(1)} %bitcast.43), channel_id=1, replica_groups=mesh['dp'=16,'fsdp'=4,'expert'=16] {'expert'}, dimensions={0} | all-to-all | bytes 1310720 | tf_op jit(solution)/shard_map/all_to_all | solution.py:275
  35.8 0.7 slice_bitcast_fusion.5
  36.5 0.0 reduce-scatter.2.cloned.1.call-start
  36.7 0.1 broadcast_in_dim.16
  36.8 34.7 %all_to_all.21.rows_ref = bf16[4,144,1280]{2,1,0:T(8,128)(2,1)S(1)} all-to-all(bf16[4,144,1280]{2,1,0:T(8,128)(2,1)S(1)} %broadcast_in_dim.16), channel_id=1, replica_groups=mesh['dp'=16,'fsdp'=4,'expert'=16] {'fsdp'}, dimensions={0} | all-to-all | bytes 2949120 | tf_op jit(solution)/shard_map/all_to_all | solution.py:278
  71.4 2.3 %forward.1 = (bf16[160,4096]{1,0:T(8,128)(2,1)}, f32[576,160]{1,0:T(8,128)}, bf16[16,4096]{1,0:T(8,128)(2,1)}, bf16[4,16,256]{2,1,0:T(8,128)(2,1)}) custom-call(bf16[4,144,1280]{2,1,0:T(8,128)(2,1)S(1)} %all_to_all.21.rows_ref, bf16[192,4096]{1,0:T(8,128)(2,1)S(1)} %bitcast.41, bf16[192,4096]{1,0:T(8,128)(2,1)S(1)} %bitcast.42), custom_call_target="tpu_custom_call" | custom-call | tf_op jit(solution)/shard_map/forward/pallas_call | solution.py:254
  73.7 3.8 %all-gather.2.cloned.1.call-done = bf16[448,1280]{1,0:T(8,128)(2,1)} async-done(((bf16[112,1280]{1,0:T(8,128)(2,1)}), bf16[448,1280]{1,0:T(8,128)(2,1)}) %all-gather.2.cloned.1.call-update) | async-done | bytes 1146896 | tf_op jit(solution)/shard_map/all_gather | solution.py:302
  77.6 5.7 %backward.1 = (bf16[576,4096]{1,0:T(8,128)(2,1)}, bf16[384,160]{1,0:T(8,128)(2,1)}) custom-call(bf16[4,112,1280]{2,1,0:T(8,128)(2,1)} %bitcast.45, bf16[16,4096]{1,0:T(8,128)(2,1)} %get-tuple-element.17.late_hbm, bf16[4,16,256]{2,1,0:T(8,128)(2,1)} %get-tuple-element.18.late_tail_hbm, bf16[192,4096]{1,0:T(8,128)(2,1)} %bitcast.44, ...), custom_call_target="tpu_custom_call" | custom-call | tf_op jit(solution)/shard_map/backward/pallas_call | solution.py:254
  83.2 0.9 copy-done.2
  84.1 0.5 fusion.3
  84.7 0.6 fusion
  85.3 0.1 slice_bitcast_fusion.3
  85.4 0.2 pad_maximum_fusion
  85.6 20.5 %all_to_all.22 = bf16[4,160,1024]{2,1,0:T(8,128)(2,1)S(1)} all-to-all(bf16[4,160,1024]{2,1,0:T(8,128)(2,1)S(1)} %pad_maximum_fusion), channel_id=1, replica_groups=mesh['dp'=16,'fsdp'=4,'expert'=16] {'fsdp'}, dimensions={0} | all-to-all | bytes 2621440 | tf_op jit(solution)/shard_map/all_to_all | solution.py:278
  106.1 0.3 convert_element_type.15
  106.4 0.2 fusion.1
  106.7 0.9 pad_maximum_fusion.1
  107.5 3.6 %all-to-all-start.3 = ((bf16[16,10,1024]{2,1,0:T(8,128)(2,1)}), bf16[16,10,1024]{2,1,0:T(8,128)(2,1)S(1)}, u32[]{:S(2)}, u32[]{:S(2)}) async-start(bf16[16,10,1024]{2,1,0:T(8,128)(2,1)} %pad_maximum_fusion.1), calls=%async_computation.3 | async-start | bytes 1048576 | tf_op jit(solution)/shard_map/all_to_all | solution.py:275
  111.1 15.9 %all-to-all-done.3 = bf16[16,10,1024]{2,1,0:T(8,128)(2,1)S(1)} async-done(((bf16[16,10,1024]{2,1,0:T(8,128)(2,1)}), bf16[16,10,1024]{2,1,0:T(8,128)(2,1)S(1)}, u32[]{:S(2)}, u32[]{:S(2)}) %all-to-all-start.3) | async-done | bytes 327712 | tf_op jit(solution)/shard_map/all_to_all | solution.py:275
  127.0 0.1 reshape.43
  127.1 1.0 convolution_convert_fusion
  128.1 40.2 %reduce-scatter.2.cloned.1.call-done.sums_hbm = bf16[576,256]{1,0:T(8,128)(2,1)} async-done(((bf16[576,4096]{1,0:T(8,128)(2,1)}), bf16[576,256]{1,0:T(8,128)(2,1)}) %reduce-scatter.2.cloned.1.call-update) | async-done | bytes 294928 | tf_op jit(solution)/shard_map/reduce_scatter | solution.py:351
  168.3 10.1 %split.1 = (bf16[192,256]{1,0:T(8,128)(2,1)}, bf16[192,256]{1,0:T(8,128)(2,1)}, bf16[192,256]{1,0:T(8,128)(2,1)}) custom-call(bf16[576,256]{1,0:T(8,128)(2,1)} %reduce-scatter.2.cloned.1.call-done.sums_hbm), custom_call_target="tpu_custom_call" | custom-call | tf_op jit(solution)/shard_map/split/pallas_call | solution.py:254
  (15 shorter events, 0.2 us)
Async XLA Ops:
  7.2 70.4 %all-gather.2.cloned.1.call-start = ((), (), s32[]{:S(2)}) async-start(), calls=%async_computation.5 | async-start | bytes 1433600 | tf_op jit(solution)/shard_map/all_gather | solution.py:302
  36.5 131.8 %reduce-scatter.2.cloned.1.call-start = ((), (), s32[]{:S(2)}) async-start(), calls=%async_computation.6 | async-start | bytes 5013504 | tf_op jit(solution)/shard_map/reduce_scatter | solution.py:351
  36.7 34.8 %copy-start.1 = (bf16[1,4096,192]{1,2,0:T(8,128)(2,1)S(1)}, bf16[1,4096,192]{1,2,0:T(8,128)(2,1)}, u32[]{:S(2)}) copy-start(bf16[1,4096,192]{1,2,0:T(8,128)(2,1)} %param.12) | copy-start | bytes 4718596
  36.8 34.7 %copy-start = (bf16[1,4096,192]{1,2,0:T(8,128)(2,1)S(1)}, bf16[1,4096,192]{1,2,0:T(8,128)(2,1)}, u32[]{:S(2)}) copy-start(bf16[1,4096,192]{1,2,0:T(8,128)(2,1)} %param.11) | copy-start | bytes 4718596
  83.2 0.9 copy-start.2
  107.5 19.5 %all-to-all-start.3 = ((bf16[16,10,1024]{2,1,0:T(8,128)(2,1)}), bf16[16,10,1024]{2,1,0:T(8,128)(2,1)S(1)}, u32[]{:S(2)}, u32[]{:S(2)}) async-start(bf16[16,10,1024]{2,1,0:T(8,128)(2,1)} %pad_maximum_fusion.1), calls=%async_computation.3 | async-start | bytes 1048576 | tf_op jit(solution)/shard_map/all_to_all | solution.py:275
Sparse Core Ops, SparseCore 0:
  36.6 40.8 all-gather.1
  83.4 84.8 reduce-scatter.1

commit v4 on v3

--- a/solution.py
+++ b/solution.py
@@ -8,7 +8,6 @@
 CAP = 10
 MAIN = 8
 TAIL = CAP - MAIN
-LATE = 16
 PIECES = MAIN // TAIL
 F32 = jnp.float32
 BF16 = jnp.bfloat16
@@ -88,31 +87,22 @@
 
 
 def forward_kernel(
-    rows_ref, gate_ref, up_ref, full_hbm, mid_hbm, late_hbm, late_tail_hbm,
-    full_ref, mid_ref, late_ref, late_tail_ref, sems,
+    rows_ref, gate_ref, up_ref, full_hbm, mid_hbm, full_ref, mid_ref, sems
 ):
-    quarters, both, _ = rows_ref.shape
-    mains = both - LATE
+    quarters, mains, _ = rows_ref.shape
     quarter = full_ref.shape[1] // quarters
     width = quarter // PIECES
     wide = gate_ref.shape[0]
     picks = [tail_pick(mains, p) for p in range(PIECES)]
     for j in range(quarters):
         low = j * quarter
-        full_ref[:mains, low : low + quarter] = rows_ref[j, :mains, :quarter]
-        packed = rows_ref[j, :mains, quarter:]
+        full_ref[:mains, low : low + quarter] = rows_ref[j, :, :quarter]
+        packed = rows_ref[j, :, quarter:]
         for p in range(PIECES):
             start = low + p * width
             full_ref[mains:, start : start + width] = dot(picks[p], packed).astype(BF16)
-        late_ref[:, low : low + quarter] = rows_ref[j, mains:, :quarter]
-        late_tail_ref[j] = rows_ref[j, mains:, quarter:]
-    keeps = [
-        pltpu.make_async_copy(full_ref, full_hbm, sems.at[0]),
-        pltpu.make_async_copy(late_ref, late_hbm, sems.at[1]),
-        pltpu.make_async_copy(late_tail_ref, late_tail_hbm, sems.at[2]),
-    ]
-    for keep in keeps:
-        keep.start()
+    keep_full = pltpu.make_async_copy(full_ref, full_hbm, sems.at[0])
+    keep_full.start()
     gate_pre = jnp.zeros((wide, full_ref.shape[0]), F32)
     up_pre = jnp.zeros((wide, full_ref.shape[0]), F32)
     for j in range(quarters):
@@ -125,18 +115,17 @@
     mid_ref[:wide, :] = up_pre * sigmoid_gate * (1.0 + gate_pre * (1.0 - sigmoid_gate))
     mid_ref[wide : 2 * wide, :] = activated
     mid_ref[2 * wide :, :] = activated * up_pre
-    keeps.append(pltpu.make_async_copy(mid_ref, mid_hbm, sems.at[3]))
-    keeps[3].start()
-    for keep in keeps:
-        keep.wait()
+    keep_mid = pltpu.make_async_copy(mid_ref, mid_hbm, sems.at[1])
+    keep_mid.start()
+    keep_full.wait()
+    keep_mid.wait()
 
 
 def backward_kernel(
-    grads_hbm, late_hbm, late_tail_hbm, down_hbm, full_hbm, mid_hbm, terms_hbm, pair_hbm,
+    grads_hbm, down_hbm, full_hbm, mid_hbm, terms_hbm, pair_hbm,
     grads_ref, tail_ref, down_ref, full_ref, mid_ref, pair_ref, pairs_ref, downs_ref, sems,
 ):
-    quarters, early, _ = grads_hbm.shape
-    mains = early + LATE
+    quarters, mains, _ = grads_hbm.shape
     quarter = full_ref.shape[1] // quarters
     width = quarter // PIECES
     wide = down_ref.shape[0]
@@ -145,17 +134,11 @@
         return ref.at[:, j * quarter : (j + 1) * quarter]
 
     mid_in = pltpu.make_async_copy(mid_hbm, mid_ref, sems.at[5, 0])
-    tail_in = pltpu.make_async_copy(
-        grads_hbm.at[:, :, quarter:], tail_ref.at[:, :early, :], sems.at[5, 1]
-    )
-    late_tail_in = pltpu.make_async_copy(
-        late_tail_hbm, tail_ref.at[:, early:, :], sems.at[5, 2]
-    )
-    late_in = pltpu.make_async_copy(late_hbm, grads_ref.at[early:mains, :], sems.at[5, 3])
+    tail_in = pltpu.make_async_copy(grads_hbm.at[:, :, quarter:], tail_ref, sems.at[5, 1])
     grads_in = [
         pltpu.make_async_copy(
             grads_hbm.at[j, :, :quarter],
-            grads_ref.at[:early, j * quarter : (j + 1) * quarter],
+            grads_ref.at[:mains, j * quarter : (j + 1) * quarter],
             sems.at[0, j],
         )
         for j in range(quarters)
@@ -169,8 +152,6 @@
         for j in range(quarters)
     ]
     tail_in.start()
-    late_tail_in.start()
-    late_in.start()
     grads_in[0].start()
     down_in[0].start()
     mid_in.start()
@@ -182,8 +163,6 @@
     picks = [tail_pick(mains, p) for p in range(PIECES)]
     hidden_grad = jnp.zeros((wide, grads_ref.shape[0]), F32)
     tail_in.wait()
-    late_tail_in.wait()
-    late_in.wait()
     outs = []
     for j in range(quarters):
         low = j * quarter
@@ -226,16 +205,22 @@
 
 
 def split_kernel(sums_hbm, *refs):
-    sems = refs[-1]
-    wide = sums_hbm.shape[0] // (len(refs) - 1)
-    copies = [
-        pltpu.make_async_copy(sums_hbm.at[i * wide : (i + 1) * wide, :], part, sems.at[i])
-        for i, part in enumerate(refs[:-1])
-    ]
-    for copy in copies:
-        copy.start()
-    for copy in copies:
-        copy.wait()
+    *parts, near_ref, sems = refs
+    wide = sums_hbm.shape[0] // len(parts)
+    loads, stores = [], []
+    for i, part in enumerate(parts):
+        block = near_ref.at[i * wide : (i + 1) * wide, :]
+        loads.append(
+            pltpu.make_async_copy(sums_hbm.at[i * wide : (i + 1) * wide, :], block, sems.at[0, i])
+        )
+        stores.append(pltpu.make_async_copy(block, part, sems.at[1, i]))
+    for load in loads:
+        load.start()
+    for load, store in zip(loads, stores):
+        load.wait()
+        store.start()
+    for store in stores:
+        store.wait()
 
 
 def vmem():
@@ -298,43 +283,37 @@
     received = to_owners(sent.reshape(owners, 2 * MAIN, packed_width))
     recv_rows = received[:, :MAIN].reshape(mains, packed_width)
     recv_grads = received[:, MAIN:].reshape(mains, packed_width)
-    early = mains - LATE
-    grads4 = lax.all_gather(recv_grads[:early], "fsdp", axis=0, tiled=True)
-    grads4 = grads4.reshape(quarters, early, packed_width)
-    near = jnp.concatenate([recv_rows, recv_grads[early:]], axis=0)
-    rows4 = to_quarters(jnp.broadcast_to(near[None], (quarters, mains + LATE, packed_width)))
+    grads4 = lax.all_gather(recv_grads, "fsdp", axis=0, tiled=True)
+    grads4 = grads4.reshape(quarters, mains, packed_width)
+    rows4 = to_quarters(jnp.broadcast_to(recv_rows[None], (quarters, mains, packed_width)))
     gate_mat = jnp.swapaxes(gate_weight, 1, 2)[0]
     up_mat = jnp.swapaxes(up_weight, 1, 2)[0]
     down_mat = down_weight[0]
     width = gate_mat.shape[0]
     tail_width = packed_width - quarter
-    full_rows, mid, late, late_tail = call(
+    full_rows, mid = call(
         forward_kernel,
         (rows4, gate_mat, up_mat),
         (
             pltpu.HBM((slots, model), BF16),
             pltpu.HBM((3 * width, slots), F32),
-            pltpu.HBM((LATE, model), BF16),
-            pltpu.HBM((quarters, LATE, tail_width), BF16),
         ),
         "forward",
         12,
-        out_specs=[hbm()] * 4,
+        out_specs=[hbm()] * 2,
         scratch=[
             pltpu.VMEM((slots, model), BF16),
             pltpu.VMEM((3 * width, slots), F32),
-            pltpu.VMEM((LATE, model), BF16),
-            pltpu.VMEM((quarters, LATE, tail_width), BF16),
-            pltpu.SemaphoreType.DMA((4,)),
+            pltpu.SemaphoreType.DMA((2,)),
         ],
     )
     terms, pair = call(
         backward_kernel,
-        far(grads4, late, late_tail, down_mat, full_rows, mid),
+        far(grads4, down_mat, full_rows, mid),
         (pltpu.HBM((3 * width, model), BF16), pltpu.HBM((2 * width, slots), BF16)),
         "backward",
         16,
-        in_specs=[hbm()] * 6,
+        in_specs=[hbm()] * 4,
         out_specs=[hbm(), hbm()],
         scratch=[
             pltpu.VMEM((slots, model), BF16),
@@ -374,7 +353,7 @@
         4,
         in_specs=[hbm()],
         out_specs=[hbm()] * 3,
-        scratch=[pltpu.SemaphoreType.DMA((3,))],
+        scratch=[pltpu.VMEM(sums.shape, BF16), pltpu.SemaphoreType.DMA((2, 3))],
     )
     return token_grads, gate_sum.T[None], up_sum.T[None], down_sum[None]
 

time: 186 us -> 178 us (0.957)
  the two profiles are of different devices: /device:TPU:2 before, /device:TPU:4 now
where the time goes in v4:
time: 178 us; the launch traced here: 177 us
  blocking collectives  74.9 us (42%)
  waiting for transfers between devices  67.2 us (38%)
  between operations  14.2 us (8%)
  Pallas kernels  11 us (6%)
  starting transfers between devices  4.42 us (2%)
  matrix products  2.09 us (1%)
  local copies, waits for them, and re-layouts  2.05 us (1%)
    all_to_all x2, blocking collectives, to_quarters(): return lax.all_to_all(x, 'fsdp', split_axis=0, concat_axis=0, tiled=True)  47.9 us
    reduce_scatter x1, waiting for transfers between devices, local(): sums = lax.psum_scatter(terms, 'dp', scatter_dimension=1, tiled=True)  42.1 us
    all_to_all x1, blocking collectives, to_owners(): return lax.all_to_all(x, 'expert', split_axis=0, concat_axis=0, tiled=True)  27 us
    all_to_all x1, waiting for transfers between devices, to_owners(): return lax.all_to_all(x, 'expert', split_axis=0, concat_axis=0, tiled=True)  15.9 us
    pallas_call x4, Pallas kernels, call(): pl.pallas_call(kernel, out_shape=outs, in_specs=in_specs if in_specs is n...  11 us
    all_gather x1, waiting for transfers between devices, local(): grads4 = lax.all_gather(recv_grads, 'fsdp', axis=0, tiled=True)  9.09 us
    all_to_all x1, starting transfers between devices, to_owners(): return lax.all_to_all(x, 'expert', split_axis=0, concat_axis=0, tiled=True)  4.34 us
  transfers between devices with their start and end apart: 3, of which 3 were waited for; matrix products, arithmetic and copies ran while one was open for 2% of the time, Pallas kernels for 1%

profile of v4, /device:TPU:4, one launch (start us, length us, event | category | flops | bytes accessed | tf_op | source)
XLA Modules:
  0.0 177.3 jit_solution(15336532556822301958)
XLA Ops:
  7.2 1.6 send.1
  8.8 27.0 %all_to_all.20 = bf16[16,16,1280]{2,1,0:T(8,128)(2,1)S(1)} all-to-all(bf16[16,16,1280]{2,1,0:T(8,128)(2,1)S(1)} %bitcast.41), channel_id=1, replica_groups=mesh['dp'=16,'fsdp'=4,'expert'=16] {'expert'}, dimensions={0} | all-to-all | bytes 1310720 | tf_op jit(solution)/shard_map/all_to_all | solution.py:260
  35.8 0.8 slice_bitcast_fusion.4
  36.6 0.0 reduce-scatter.2.cloned.1.call-start
  36.6 0.1 broadcast_in_dim.18
  36.7 28.8 %all_to_all.21.rows_ref = bf16[4,128,1280]{2,1,0:T(8,128)(2,1)S(1)} all-to-all(bf16[4,128,1280]{2,1,0:T(8,128)(2,1)S(1)} %broadcast_in_dim.18), channel_id=1, replica_groups=mesh['dp'=16,'fsdp'=4,'expert'=16] {'fsdp'}, dimensions={0} | all-to-all | bytes 2621440 | tf_op jit(solution)/shard_map/all_to_all | solution.py:263
  65.5 2.2 %forward.1 = (bf16[160,4096]{1,0:T(8,128)(2,1)}, f32[576,160]{1,0:T(8,128)}) custom-call(bf16[4,128,1280]{2,1,0:T(8,128)(2,1)S(1)} %all_to_all.21.rows_ref, bf16[192,4096]{1,0:T(8,128)(2,1)S(1)} %bitcast.39, bf16[192,4096]{1,0:T(8,128)(2,1)S(1)} %bitcast.40), custom_call_target="tpu_custom_call" | custom-call | tf_op jit(solution)/shard_map/forward/pallas_call | solution.py:239
  67.7 9.1 %all-gather.2.cloned.1.call-done = bf16[512,1280]{1,0:T(8,128)(2,1)} async-done(((bf16[128,1280]{1,0:T(8,128)(2,1)}), bf16[512,1280]{1,0:T(8,128)(2,1)}) %all-gather.2.cloned.1.call-update) | async-done | bytes 1310736 | tf_op jit(solution)/shard_map/all_gather | solution.py:286
  76.8 5.5 %backward.1 = (bf16[576,4096]{1,0:T(8,128)(2,1)}, bf16[384,160]{1,0:T(8,128)(2,1)}) custom-call(bf16[4,128,1280]{2,1,0:T(8,128)(2,1)} %bitcast.43, bf16[192,4096]{1,0:T(8,128)(2,1)} %bitcast.42, bf16[160,4096]{1,0:T(8,128)(2,1)} %get-tuple-element.15.full_hbm, f32[576,160]{1,0:T(8,128)} %get-tuple-element.16.mid_hbm), custom_call_target="tpu_custom_call" | custom-call | tf_op jit(solution)/shard_map/backward/pallas_call | solution.py:239
  82.3 0.9 copy-done.2
  83.2 0.5 fusion.3
  83.8 0.6 fusion
  84.4 0.1 slice_bitcast_fusion.3
  84.5 0.2 pad_maximum_fusion
  84.7 19.2 %all_to_all.22 = bf16[4,160,1024]{2,1,0:T(8,128)(2,1)S(1)} all-to-all(bf16[4,160,1024]{2,1,0:T(8,128)(2,1)S(1)} %pad_maximum_fusion), channel_id=1, replica_groups=mesh['dp'=16,'fsdp'=4,'expert'=16] {'fsdp'}, dimensions={0} | all-to-all | bytes 2621440 | tf_op jit(solution)/shard_map/all_to_all | solution.py:263
  103.8 0.3 convert_element_type.15
  104.1 0.2 fusion.1
  104.4 0.9 pad_maximum_fusion.1
  105.3 4.3 %all-to-all-start.3 = ((bf16[16,10,1024]{2,1,0:T(8,128)(2,1)}), bf16[16,10,1024]{2,1,0:T(8,128)(2,1)S(1)}, u32[]{:S(2)}, u32[]{:S(2)}) async-start(bf16[16,10,1024]{2,1,0:T(8,128)(2,1)} %pad_maximum_fusion.1), calls=%async_computation.3 | async-start | bytes 1048576 | tf_op jit(solution)/shard_map/all_to_all | solution.py:260
  109.6 15.9 %all-to-all-done.3 = bf16[16,10,1024]{2,1,0:T(8,128)(2,1)S(1)} async-done(((bf16[16,10,1024]{2,1,0:T(8,128)(2,1)}), bf16[16,10,1024]{2,1,0:T(8,128)(2,1)S(1)}, u32[]{:S(2)}, u32[]{:S(2)}) %all-to-all-start.3) | async-done | bytes 327712 | tf_op jit(solution)/shard_map/all_to_all | solution.py:260
  125.6 0.1 reshape.40
  125.7 1.0 convolution_convert_fusion
  126.7 42.1 %reduce-scatter.2.cloned.1.call-done.sums_hbm = bf16[576,256]{1,0:T(8,128)(2,1)} async-done(((bf16[576,4096]{1,0:T(8,128)(2,1)}), bf16[576,256]{1,0:T(8,128)(2,1)}) %reduce-scatter.2.cloned.1.call-update) | async-done | bytes 294928 | tf_op jit(solution)/shard_map/reduce_scatter | solution.py:330
  168.8 1.7 split.1
  (12 shorter events, 0.1 us)
Async XLA Ops:
  7.2 69.7 %all-gather.2.cloned.1.call-start = ((), (), s32[]{:S(2)}) async-start(), calls=%async_computation.5 | async-start | bytes 1638400 | tf_op jit(solution)/shard_map/all_gather | solution.py:286
  36.6 132.2 %reduce-scatter.2.cloned.1.call-start = ((), (), s32[]{:S(2)}) async-start(), calls=%async_computation.6 | async-start | bytes 5013504 | tf_op jit(solution)/shard_map/reduce_scatter | solution.py:330
  36.6 28.9 %copy-start.1 = (bf16[1,4096,192]{1,2,0:T(8,128)(2,1)S(1)}, bf16[1,4096,192]{1,2,0:T(8,128)(2,1)}, u32[]{:S(2)}) copy-start(bf16[1,4096,192]{1,2,0:T(8,128)(2,1)} %param.12) | copy-start | bytes 4718596
  36.7 28.8 %copy-start = (bf16[1,4096,192]{1,2,0:T(8,128)(2,1)S(1)}, bf16[1,4096,192]{1,2,0:T(8,128)(2,1)}, u32[]{:S(2)}) copy-start(bf16[1,4096,192]{1,2,0:T(8,128)(2,1)} %param.11) | copy-start | bytes 4718596
  82.3 0.9 copy-start.2
  105.3 20.3 %all-to-all-start.3 = ((bf16[16,10,1024]{2,1,0:T(8,128)(2,1)}), bf16[16,10,1024]{2,1,0:T(8,128)(2,1)S(1)}, u32[]{:S(2)}, u32[]{:S(2)}) async-start(bf16[16,10,1024]{2,1,0:T(8,128)(2,1)} %pad_maximum_fusion.1), calls=%async_computation.3 | async-start | bytes 1048576 | tf_op jit(solution)/shard_map/all_to_all | solution.py:260
Sparse Core Ops, SparseCore 0:
  36.7 40.1 all-gather.1
  82.5 86.2 reduce-scatter.1

commit v5 on v4

--- a/solution.py
+++ b/solution.py
@@ -80,10 +80,19 @@
     out_ref[:, quarter:] = tail.astype(BF16)
 
 
-def tail_pick(rows, p):
+def tail_pick(rows):
     tails = rows // MAIN * TAIL
-    slot, row = iota((tails, rows), 0), iota((tails, rows), 1)
-    return (row == slot // TAIL * MAIN + slot % TAIL * PIECES + p).astype(BF16)
+    out, row = iota((tails * PIECES, rows), 0), iota((tails * PIECES, rows), 1)
+    slot, piece = out % tails, out // tails
+    return (row == slot // TAIL * MAIN + slot % TAIL * PIECES + piece).astype(BF16)
+
+
+def unpack_tail(pick, packed, ref, mains, low):
+    tails, width = ref.shape[0] - mains, packed.shape[1]
+    pieces = dot(pick, packed).astype(BF16)
+    for p in range(PIECES):
+        start = low + p * width
+        ref[mains:, start : start + width] = pieces[p * tails : (p + 1) * tails]
 
 
 def forward_kernel(
@@ -91,16 +100,12 @@
 ):
     quarters, mains, _ = rows_ref.shape
     quarter = full_ref.shape[1] // quarters
-    width = quarter // PIECES
     wide = gate_ref.shape[0]
-    picks = [tail_pick(mains, p) for p in range(PIECES)]
+    pick = tail_pick(mains)
     for j in range(quarters):
         low = j * quarter
         full_ref[:mains, low : low + quarter] = rows_ref[j, :, :quarter]
-        packed = rows_ref[j, :, quarter:]
-        for p in range(PIECES):
-            start = low + p * width
-            full_ref[mains:, start : start + width] = dot(picks[p], packed).astype(BF16)
+        unpack_tail(pick, rows_ref[j, :, quarter:], full_ref, mains, low)
     keep_full = pltpu.make_async_copy(full_ref, full_hbm, sems.at[0])
     keep_full.start()
     gate_pre = jnp.zeros((wide, full_ref.shape[0]), F32)
@@ -127,7 +132,6 @@
 ):
     quarters, mains, _ = grads_hbm.shape
     quarter = full_ref.shape[1] // quarters
-    width = quarter // PIECES
     wide = down_ref.shape[0]
 
     def columns(ref, j):
@@ -160,15 +164,13 @@
         down_in[j].start()
     for j in range(quarters):
         full_in[j].start()
-    picks = [tail_pick(mains, p) for p in range(PIECES)]
+    pick = tail_pick(mains)
     hidden_grad = jnp.zeros((wide, grads_ref.shape[0]), F32)
     tail_in.wait()
     outs = []
     for j in range(quarters):
         low = j * quarter
-        for p in range(PIECES):
-            start = low + p * width
-            grads_ref[mains:, start : start + width] = dot(picks[p], tail_ref[j]).astype(BF16)
+        unpack_tail(pick, tail_ref[j], grads_ref, mains, low)
         grads_in[j].wait()
         down_in[j].wait()
         block = grads_ref[:, low : low + quarter]

time: 178 us -> 177 us (level)
  the two profiles are of different devices: /device:TPU:4 before, /device:TPU:18 now
where the time goes in v5:
time: 177 us
  blocking collectives  74.6 us (42%)
  waiting for transfers between devices  65 us (37%)
  between operations  14.2 us (8%)
  Pallas kernels  11 us (6%)
  starting transfers between devices  6.63 us (4%)
  matrix products  2.07 us (1%)
  local copies, waits for them, and re-layouts  2.05 us (1%)
    all_to_all x2, blocking collectives, to_quarters(): return lax.all_to_all(x, 'fsdp', split_axis=0, concat_axis=0, tiled=True)  49.1 us
    reduce_scatter x1, waiting for transfers between devices, local(): sums = lax.psum_scatter(terms, 'dp', scatter_dimension=1, tiled=True)  41.3 us
    all_to_all x1, blocking collectives, to_owners(): return lax.all_to_all(x, 'expert', split_axis=0, concat_axis=0, tiled=True)  25.5 us
    all_to_all x1, waiting for transfers between devices, to_owners(): return lax.all_to_all(x, 'expert', split_axis=0, concat_axis=0, tiled=True)  14.9 us
    pallas_call x4, Pallas kernels, call(): pl.pallas_call(kernel, out_shape=outs, in_specs=in_specs if in_specs is n...  11 us
    all_gather x1, waiting for transfers between devices, local(): grads4 = lax.all_gather(recv_grads, 'fsdp', axis=0, tiled=True)  8.77 us
    all_to_all x1, starting transfers between devices, to_owners(): return lax.all_to_all(x, 'expert', split_axis=0, concat_axis=0, tiled=True)  6.55 us
  transfers between devices with their start and end apart: 3, of which 3 were waited for; matrix products, arithmetic and copies ran while one was open for 2% of the time, Pallas kernels for 1%

profile of v5, /device:TPU:18, one launch (start us, length us, event | category | flops | bytes accessed | tf_op | source)
XLA Modules:
  0.0 177.0 jit_solution(33181153772031201)
XLA Ops:
  7.2 1.6 send.1
  8.8 25.5 %all_to_all.20 = bf16[16,16,1280]{2,1,0:T(8,128)(2,1)S(1)} all-to-all(bf16[16,16,1280]{2,1,0:T(8,128)(2,1)S(1)} %bitcast.41), channel_id=1, replica_groups=mesh['dp'=16,'fsdp'=4,'expert'=16] {'expert'}, dimensions={0} | all-to-all | bytes 1310720 | tf_op jit(solution)/shard_map/all_to_all | solution.py:262
  34.3 0.8 slice_bitcast_fusion.4
  35.1 0.0 reduce-scatter.2.cloned.1.call-start
  35.1 0.1 broadcast_in_dim.18
  35.2 28.6 %all_to_all.21.rows_ref = bf16[4,128,1280]{2,1,0:T(8,128)(2,1)S(1)} all-to-all(bf16[4,128,1280]{2,1,0:T(8,128)(2,1)S(1)} %broadcast_in_dim.18), channel_id=1, replica_groups=mesh['dp'=16,'fsdp'=4,'expert'=16] {'fsdp'}, dimensions={0} | all-to-all | bytes 2621440 | tf_op jit(solution)/shard_map/all_to_all | solution.py:265
  63.9 2.2 %forward.1 = (bf16[160,4096]{1,0:T(8,128)(2,1)}, f32[576,160]{1,0:T(8,128)}) custom-call(bf16[4,128,1280]{2,1,0:T(8,128)(2,1)S(1)} %all_to_all.21.rows_ref, bf16[192,4096]{1,0:T(8,128)(2,1)S(1)} %bitcast.39, bf16[192,4096]{1,0:T(8,128)(2,1)S(1)} %bitcast.40), custom_call_target="tpu_custom_call" | custom-call | tf_op jit(solution)/shard_map/forward/pallas_call | solution.py:241
  66.1 8.8 %all-gather.2.cloned.1.call-done = bf16[512,1280]{1,0:T(8,128)(2,1)} async-done(((bf16[128,1280]{1,0:T(8,128)(2,1)}), bf16[512,1280]{1,0:T(8,128)(2,1)}) %all-gather.2.cloned.1.call-update) | async-done | bytes 1310736 | tf_op jit(solution)/shard_map/all_gather | solution.py:288
  74.8 5.5 %backward.1 = (bf16[576,4096]{1,0:T(8,128)(2,1)}, bf16[384,160]{1,0:T(8,128)(2,1)}) custom-call(bf16[4,128,1280]{2,1,0:T(8,128)(2,1)} %bitcast.43, bf16[192,4096]{1,0:T(8,128)(2,1)} %bitcast.42, bf16[160,4096]{1,0:T(8,128)(2,1)} %get-tuple-element.15.full_hbm, f32[576,160]{1,0:T(8,128)} %get-tuple-element.16.mid_hbm), custom_call_target="tpu_custom_call" | custom-call | tf_op jit(solution)/shard_map/backward/pallas_call | solution.py:241
  80.4 0.9 copy-done.2
  81.3 0.5 fusion.3
  81.8 0.6 fusion
  82.4 0.1 slice_bitcast_fusion.3
  82.5 0.2 pad_maximum_fusion
  82.7 20.5 %all_to_all.22 = bf16[4,160,1024]{2,1,0:T(8,128)(2,1)S(1)} all-to-all(bf16[4,160,1024]{2,1,0:T(8,128)(2,1)S(1)} %pad_maximum_fusion), channel_id=1, replica_groups=mesh['dp'=16,'fsdp'=4,'expert'=16] {'fsdp'}, dimensions={0} | all-to-all | bytes 2621440 | tf_op jit(solution)/shard_map/all_to_all | solution.py:265
  103.2 0.3 convert_element_type.15
  103.5 0.2 fusion.1
  103.7 0.9 pad_maximum_fusion.1
  104.6 6.6 %all-to-all-start.3 = ((bf16[16,10,1024]{2,1,0:T(8,128)(2,1)}), bf16[16,10,1024]{2,1,0:T(8,128)(2,1)S(1)}, u32[]{:S(2)}, u32[]{:S(2)}) async-start(bf16[16,10,1024]{2,1,0:T(8,128)(2,1)} %pad_maximum_fusion.1), calls=%async_computation.3 | async-start | bytes 1048576 | tf_op jit(solution)/shard_map/all_to_all | solution.py:262
  111.2 14.9 %all-to-all-done.3 = bf16[16,10,1024]{2,1,0:T(8,128)(2,1)S(1)} async-done(((bf16[16,10,1024]{2,1,0:T(8,128)(2,1)}), bf16[16,10,1024]{2,1,0:T(8,128)(2,1)S(1)}, u32[]{:S(2)}, u32[]{:S(2)}) %all-to-all-start.3) | async-done | bytes 327712 | tf_op jit(solution)/shard_map/all_to_all | solution.py:262
  126.1 0.1 reshape.40
  126.2 1.0 convolution_convert_fusion
  127.2 41.3 %reduce-scatter.2.cloned.1.call-done.sums_hbm = bf16[576,256]{1,0:T(8,128)(2,1)} async-done(((bf16[576,4096]{1,0:T(8,128)(2,1)}), bf16[576,256]{1,0:T(8,128)(2,1)}) %reduce-scatter.2.cloned.1.call-update) | async-done | bytes 294928 | tf_op jit(solution)/shard_map/reduce_scatter | solution.py:332
  168.5 1.7 split.1
  (12 shorter events, 0.1 us)
Async XLA Ops:
  7.2 67.7 %all-gather.2.cloned.1.call-start = ((), (), s32[]{:S(2)}) async-start(), calls=%async_computation.5 | async-start | bytes 1638400 | tf_op jit(solution)/shard_map/all_gather | solution.py:288
  35.1 133.4 %reduce-scatter.2.cloned.1.call-start = ((), (), s32[]{:S(2)}) async-start(), calls=%async_computation.6 | async-start | bytes 5013504 | tf_op jit(solution)/shard_map/reduce_scatter | solution.py:332
  35.1 28.7 %copy-start.1 = (bf16[1,4096,192]{1,2,0:T(8,128)(2,1)S(1)}, bf16[1,4096,192]{1,2,0:T(8,128)(2,1)}, u32[]{:S(2)}) copy-start(bf16[1,4096,192]{1,2,0:T(8,128)(2,1)} %param.12) | copy-start | bytes 4718596
  35.2 28.6 %copy-start = (bf16[1,4096,192]{1,2,0:T(8,128)(2,1)S(1)}, bf16[1,4096,192]{1,2,0:T(8,128)(2,1)}, u32[]{:S(2)}) copy-start(bf16[1,4096,192]{1,2,0:T(8,128)(2,1)} %param.11) | copy-start | bytes 4718596
  80.4 0.9 copy-start.2
  104.6 21.4 %all-to-all-start.3 = ((bf16[16,10,1024]{2,1,0:T(8,128)(2,1)}), bf16[16,10,1024]{2,1,0:T(8,128)(2,1)S(1)}, u32[]{:S(2)}, u32[]{:S(2)}) async-start(bf16[16,10,1024]{2,1,0:T(8,128)(2,1)} %pad_maximum_fusion.1), calls=%async_computation.3 | async-start | bytes 1048576 | tf_op jit(solution)/shard_map/all_to_all | solution.py:262
Sparse Core Ops, SparseCore 0:
  35.2 39.5 all-gather.1
  80.5 87.9 reduce-scatter.1
